TPU v7x, 32 devices: a whole 2x2x4 slice. The times are simulated.
32 devices in a mesh: col: 4 (over z), row: 8 (over y, x, core).
Axes of the slice: x: 2, y: 2, z: 4, core: 2. Of those that a mesh axis runs over, the one named last changes fastest.
Arguments:
- matrix: bfloat16 [24576, 24576], P('row', 'col'), may hold values from -9 to 9
- left_basis: float32 [320, 24576], P(None, ('row', 'col')), may hold values from -6 to 6
- right_basis: float32 [320, 24576], P(None, ('col', 'row')), may hold values from -6 to 6
- right_block: float32 [64, 24576], P(None, ('col', 'row')), may hold values from -6 to 6
Outputs:
- left_blocks: float32 [64, 24576], P(None, ('row', 'col'))
- right_blocks: float32 [64, 24576], P(None, ('col', 'row'))
- factors: float32 [2, 64, 64], replicated
All inputs are finite; a program needn't handle non-finite values.
Results may differ from a plain program's by a relative error of at most 0.0041.
Values may be sent and summed in bfloat16 or wider, within the bound.
No kernel may reach another device: no remote copies, remote signals or barrier semaphores. Data moves between devices by JAX's collectives and lax.ppermute only.
A program may use at most 128 MiB of HBM per device.

v0:
```python
import functools

import jax
import jax.numpy as jnp
from jax import lax
from jax.experimental import pallas as pl
from jax.experimental.pallas import tpu as pltpu
from jax.sharding import PartitionSpec as P


f32 = jnp.float32
bf16 = jnp.bfloat16
CROSS = bf16
TILE = 128
ANY = pl.BlockSpec(memory_space=pltpu.HBM)
VMEM = pl.BlockSpec(memory_space=pltpu.VMEM)


def dot16(first, second, dims):
    return lax.dot_general(first, second, (dims, ((), ())), preferred_element_type=f32)


def dot32(first, second, dims):
    return lax.dot_general(first, second, (dims, ((), ())), precision=lax.Precision.HIGHEST, preferred_element_type=f32)


def split(values):
    high = values.astype(bf16)
    return high, (values - high.astype(f32)).astype(bf16)


def limit(mebibytes):
    return pltpu.CompilerParams(vmem_limit_bytes=mebibytes << 20)


def shape(dims, dtype=f32):
    return jax.ShapeDtypeStruct(dims, dtype)


def padded(count):
    return -(-count // 128) * 128


def call(kernel, inputs, outputs, specs=None, scratch=(), mebibytes=8):
    return pl.pallas_call(
        kernel,
        in_specs=specs or [VMEM] * len(inputs),
        out_specs=[VMEM] * len(outputs),
        out_shape=outputs,
        scratch_shapes=list(scratch),
        compiler_params=limit(mebibytes),
    )(*inputs)


def swap(values, axis, size, bit):
    return lax.ppermute(values, axis, [(i, i ^ bit) for i in range(size)])


def exchange_sum(values, axis, size, bit):
    while bit < size:
        if bit * 2 < size:
            one, two, three = (swap(values, axis, size, m) for m in (bit, bit * 2, bit * 3))
            values = (values + one) + (two + three)
            bit *= 4
        else:
            values = values + swap(values, axis, size, bit)
            bit *= 2
    return values


HALVES = 2


def fetch_copies(a_hbm, targets, sems, chunks, chunk):
    me = lax.axis_index("col")
    part = chunk // HALVES
    copies = []
    for n, j in enumerate(chunks):
        for h in range(HALVES):
            start = pl.multiple_of((me ^ j) * chunk + h * part, part)
            copies.append(
                pltpu.make_async_copy(
                    a_hbm.at[pl.ds(start, part), :], targets[n].at[pl.ds(h * part, part), :], sems.at[n, h]
                )
            )
    return copies


def fetch(matrix, chunk, j):
    def kernel(a_hbm, target, sems):
        copies = fetch_copies(a_hbm, [target], sems, [j], chunk)
        for copy in copies:
            copy.start()
        for copy in copies:
            copy.wait()

    outputs = [shape((chunk, matrix.shape[1]), bf16)]
    return call(kernel, [matrix], outputs, specs=[ANY], scratch=[pltpu.SemaphoreType.DMA((1, HALVES))], mebibytes=24)[0]


def prepare(bases, gram_total=None):
    width = bases[0].shape[1]
    total = sum(b.shape[0] for b in bases)
    size = padded(total)

    def kernel(*rest):
        sources, (rows_high, rows_low, turned) = rest[: len(bases)], rest[len(bases) : len(bases) + 3]
        if total != size:
            rows_high[...] = jnp.zeros_like(rows_high)
            rows_low[...] = jnp.zeros_like(rows_low)
            turned[...] = jnp.zeros_like(turned)
        at = 0
        for source in sources:
            values = source[...]
            count = values.shape[0]
            high, low = split(values)
            rows_high[at : at + count, :] = high
            rows_low[at : at + count, :] = low
            high, low = split(values.T)
            turned[:, at : at + count] = high
            turned[:, size + at : size + at + count] = low
            at += count
        if gram_total is not None:
            mine, theirs, held = rest[len(bases) + 3 :]
            gram = dot16(rows_high[...], turned[...], ((1,), (0,)))
            gram = gram[:, :size] + (gram[:, size:] + dot16(rows_low[...], turned[:, :size], ((1,), (0,))))
            gram = gram * (1.0 / gram_total)
            held[:TILE, :TILE] = gram[:TILE, :TILE]
            held[:TILE, TILE:] = gram[TILE : 2 * TILE, : 2 * TILE]
            held[TILE:, :] = gram[2 * TILE :, :]
            own = lax.axis_index("row") % 2
            mine[...] = held[pl.ds(pl.multiple_of(own * TILE, TILE), TILE), :]
            theirs[...] = held[pl.ds(pl.multiple_of((1 - own) * TILE, TILE), TILE), :]

    outputs = [shape((size, width), bf16), shape((size, width), bf16), shape((width, 2 * size), bf16)]
    scratch = []
    if gram_total is not None:
        outputs += [shape((TILE, size))] * 2
        scratch = [pltpu.VMEM((2 * TILE, size), f32)]
    return call(kernel, list(bases), outputs, scratch=scratch)


def quarter_sums(mine, theirs):
    rows = mine.shape[0] // 4

    def kernel(mine_ref, theirs_ref, *rest):
        outs, held = rest[:4], rest[4]
        held[...] = mine_ref[...] + theirs_ref[...]
        chip = lax.axis_index("row") // 2
        for k, out in enumerate(outs):
            out[...] = held[pl.ds(pl.multiple_of((chip ^ k) * rows, rows), rows), :]

    return call(kernel, [mine, theirs], [shape((rows, mine.shape[1]))] * 4, scratch=[pltpu.VMEM(mine.shape, f32)])


def fold(parts):
    def kernel(a, b, c, d, out):
        out[...] = (a[...] + b[...]) + (c[...] + d[...])

    return call(kernel, list(parts), [shape(parts[0].shape)])[0]


def pair(own_part, other_part):
    rows = own_part.shape[0]

    def kernel(own_ref, other_ref, out_ref):
        own = lax.axis_index("row") % 2
        out_ref[pl.ds(pl.multiple_of(own * rows, rows), rows), :] = own_ref[...]
        out_ref[pl.ds(pl.multiple_of((1 - own) * rows, rows), rows), :] = other_ref[...]

    return call(kernel, [own_part, other_part], [shape((2 * rows, own_part.shape[1]))])[0]


def forward(lefts, order, held, matrix, chunk, products, brought):
    cols = matrix.shape[1]
    block = lefts[0].shape[0]
    step = chunk // 3 if chunk % 384 == 0 else chunk
    source = [matrix] if brought else []

    def kernel(*rest):
        rest = list(rest)
        parts = [rest.pop(0) for _ in lefts]
        chunks = {j: rest.pop(0) for j in held}
        a_hbm = [rest.pop(0) for _ in source]
        outs = [rest.pop(0) for _ in products]
        targets = [rest.pop(0) for _ in brought]
        copies = fetch_copies(a_hbm[0], targets, rest[-1], brought, chunk) if brought else []
        for copy in copies:
            copy.start()
        if order is None:
            whole = parts[0]
        else:
            whole = rest.pop(0)
            me = lax.axis_index("row")
            width = parts[0].shape[1]
            for part, m in zip(parts, order):
                whole[:, pl.ds(pl.multiple_of((me ^ m) * width, width), width)] = part[...]
        waited = 0
        for j, out in zip(products, outs):
            if j not in chunks:
                at = brought.index(j)
                for copy in copies[waited : HALVES * (at + 1)]:
                    copy.wait()
                waited = HALVES * (at + 1)
                chunks[j] = targets[at]
            right = chunks[j]

            def one(n, _, right=right, out=out):
                at = pl.ds(pl.multiple_of(n * step, step), step)
                out[:, at] = dot16(whole[...], right[at, :], ((1,), (1,))).astype(out.dtype)
                return _

            lax.fori_loop(0, chunk // step, one, 0)
        for copy in copies[waited:]:
            copy.wait()

    outputs = [shape((block, chunk), f32 if j == 0 else CROSS) for j in products]
    outputs += [shape((chunk, cols), bf16) for _ in brought]
    if order is not None:
        outputs.append(shape((block, cols), bf16))
    return call(
        kernel,
        list(lefts) + list(held.values()) + source,
        outputs,
        specs=[VMEM] * (len(lefts) + len(held)) + [ANY] * len(source),
        scratch=[pltpu.SemaphoreType.DMA((len(brought), HALVES))] if brought else [],
        mebibytes=8,
    )


def backward_begin(piece, chunk_j, begun=None):
    given = [] if begun is None else [begun]

    def kernel(p_ref, a_ref, *rest):
        got = dot16(p_ref[...], a_ref[...], ((1,), (0,)))
        rest[-1][...] = rest[0][...] + got if given else got

    return call(kernel, [piece, chunk_j, *given], [shape((piece.shape[0], chunk_j.shape[1]))])[0]


def backward(pieces, chunks, begun, targets, parts):
    groups = len(pieces)
    block = pieces[0].shape[0]
    width = chunks[0].shape[1] // parts

    def kernel(*rest):
        lefts, rights, begun_ref, outs = rest[:groups], rest[groups : 2 * groups], rest[2 * groups], rest[2 * groups + 1 :]
        me = lax.axis_index("row")
        for out, wanted in zip(outs, targets):
            for n, j in enumerate(wanted):
                at = pl.ds(pl.multiple_of((me ^ j) * width, width), width)
                total = begun_ref[:, at]
                for left, right in zip(lefts, rights):
                    total = total + dot16(left[...], right[:, at], ((1,), (0,)))
                out[n] = total

    outputs = [shape((len(wanted), block, width)) for wanted in targets]
    return call(kernel, [*pieces, *chunks, begun], outputs)


def combine(mine, theirs):
    count, block, width = mine.shape

    def kernel(mine_ref, theirs_ref, *outs):
        for n, out in enumerate(outs):
            out[...] = (mine_ref[n] + theirs_ref[n]).astype(CROSS)

    return call(kernel, [mine, theirs], [shape((block, width), CROSS)] * count)


def coefficients(pieces, turned, total, further=None, with_gram=False):
    block, width = pieces[0].shape[-2:]
    size = turned.shape[1] // 2
    half = block // 2
    n_pieces = len(pieces)
    given = [] if further is None else [further]
    count = size + (further.shape[1] if given else 0) + (block if with_gram else 0)

    def kernel(*rest):
        parts, turned_ref = rest[:n_pieces], rest[n_pieces]
        more = rest[n_pieces + 1 : n_pieces + 1 + len(given)]
        image_ref, mine_ref, theirs_ref, held = rest[n_pieces + 1 + len(given) :]
        image = parts[0][...].astype(f32).reshape(block, width)
        for part in parts[1:]:
            image = image + part[...].astype(f32).reshape(block, width)
        image_ref[...] = image
        high, low = split(image)
        right = turned_ref[...]
        got = dot16(high, right, ((1,), (0,)))
        got = got[:, :size] + (got[:, size:] + dot16(low, right[:, :size], ((1,), (0,))))
        held[:, :size] = got * (1.0 / total)
        if more:
            held[:, size : size + more[0].shape[1]] = more[0][...]
        if with_gram:
            cross = dot16(high, low, ((1,), (1,))) + dot16(low, high, ((1,), (1,)))
            held[:, count - block :] = (dot16(high, high, ((1,), (1,))) + cross) * (1.0 / total)
        own = lax.axis_index("row") % 2
        mine_ref[...] = held[pl.ds(pl.multiple_of(own * half, half), half), :]
        theirs_ref[...] = held[pl.ds(pl.multiple_of((1 - own) * half, half), half), :]

    return call(
        kernel,
        [*pieces, turned, *given],
        [shape((block, width)), shape((half, count)), shape((half, count))],
        scratch=[pltpu.VMEM((block, count), f32)],
    )


def project(image, rows_high, rows_low, mine, other, total):
    block, width = image.shape
    size = rows_high.shape[0]
    half = block // 2
    count = mine.shape[1]

    def kernel(image_ref, high_ref, low_ref, mine_ref, other_ref, *rest):
        out_ref, round_ref, gram_ref = rest[:3]
        held = rest[-1]
        own = lax.axis_index("row") % 2
        held[pl.ds(pl.multiple_of(own * half, half), half), :] = mine_ref[...]
        held[pl.ds(pl.multiple_of((1 - own) * half, half), half), :] = other_ref[...]
        high, low = split(held[:, :size])
        right = high_ref[...]
        taken = dot16(high, right, ((1,), (0,))) + (
            dot16(low, right, ((1,), (0,))) + dot16(high, low_ref[...], ((1,), (0,)))
        )
        out = image_ref[...] - taken
        high, low = split(out)
        out_ref[...] = out
        round_ref[...] = high
        cross = dot16(high, low, ((1,), (1,))) + dot16(low, high, ((1,), (1,)))
        gram_ref[...] = (dot16(high, high, ((1,), (1,))) + cross) * (1.0 / total)
        if count > size:
            rest[3][...] = held[:, size:]

    outputs = [shape((block, width)), shape((block, width), bf16), shape((block, block))]
    if count > size:
        outputs.append(shape((block, count - size)))
    return call(kernel, [image, rows_high, rows_low, mine, other], outputs, scratch=[pltpu.VMEM((block, count), f32)])


GROUP = 8
JOINT = 8


def eliminate_all(grams, group):
    block = grams[0].shape[0]
    line = lax.broadcasted_iota(jnp.int32, (block, block), 0)
    lane = lax.broadcasted_iota(jnp.int32, (block, block), 1)
    unit = jnp.where(line == lane, 1.0, 0.0).astype(f32)
    all_both = [jnp.concatenate([gram, unit], 1) for gram in grams]
    place = lax.broadcasted_iota(jnp.int32, all_both[0].shape, 0)
    for base in range(0, block, group):
        count = min(group, block - base)
        spread = [
            [jnp.broadcast_to(both[:, base + q : base + q + 1], both.shape) for q in range(count)] for both in all_both
        ]
        for q in range(count):
            j = base + q
            for n, columns in enumerate(spread):
                pivot = 1.0 / columns[q][j : j + 1, :]
                ratio = jnp.where(place > j, columns[q] * pivot, 0.0)
                for p in range(q + 1, count):
                    columns[p] = columns[p] - ratio * columns[p][j : j + 1, :]
                all_both[n] = all_both[n] - ratio * all_both[n][j : j + 1, :]
    found = []
    for both in all_both:
        upper = both[:, :block]
        diagonal = jnp.sum(jnp.where(line == lane, upper, 0.0), axis=1, keepdims=True)
        scale = 1.0 / jnp.sqrt(diagonal)
        inverse = jnp.where(line >= lane, both[:, block:] * scale, 0.0)
        found.append((jnp.where(lane >= line, upper * scale, 0.0).T, inverse))
    return found


def eliminate(gram):
    return eliminate_all([gram], GROUP)[0]


def finish(image, rows_high, rows_low, mine, other, quarters, left_rows):
    block, width = image.shape
    size = rows_high.shape[0]
    half = block // 2
    count = mine.shape[1]
    rows = quarters[0].shape[0] // 2

    def kernel(image_ref, high_ref, low_ref, mine_ref, other_ref, q0, q1, q2, q3, left_ref, *rest):
        left_new_ref, right_new_ref, factors_ref, held, near, far = rest
        own = lax.axis_index("row") % 2
        chip = lax.axis_index("row") // 2
        held[pl.ds(pl.multiple_of(own * half, half), half), :] = mine_ref[...]
        held[pl.ds(pl.multiple_of((1 - own) * half, half), half), :] = other_ref[...]
        for k, quarter in enumerate((q0, q1, q2, q3)):
            at = pl.ds(pl.multiple_of((chip ^ k) * rows, rows), rows)
            near[at, :] = quarter[:rows, :]
            far[at, :] = quarter[rows:, :]
        coefs = held[:, :size]
        first, second, third = (coefs[:, n * TILE : (n + 1) * TILE] for n in range(3))
        by_row = ((1,), (0,))
        last = dot32(third, far[...], by_row)
        middle = dot32(second, near[:, TILE:], by_row)
        start = 0.5 * dot32(first, near[:, :TILE], by_row) + middle[:, :TILE] + last[:, :TILE]
        middle = 0.5 * middle[:, TILE:] + last[:, TILE : 2 * TILE]
        weighted = jnp.concatenate([start - first, middle - second, 0.5 * last[:, 2 * TILE :] - third], 1)
        weighted = dot32(weighted, coefs, ((1,), (1,)))
        left_gram = held[:, size : size + block]
        right_gram = held[:, size + block :] + (weighted + weighted.T)

        high, low = split(coefs)
        right = high_ref[...]
        taken = dot16(high, right, by_row) + (dot16(low, right, by_row) + dot16(high, low_ref[...], by_row))
        projected = image_ref[...] - taken
        (left_low, left_inverse), (right_low, right_inverse) = eliminate_all([left_gram, right_gram], JOINT)
        right_new_ref[...] = dot32(right_inverse, projected, by_row)
        left_new_ref[...] = dot32(left_inverse, left_ref[...], by_row)
        line = lax.broadcasted_iota(jnp.int32, (block, block), 0)
        lane = lax.broadcasted_iota(jnp.int32, (block, block), 1)
        factors_ref[0] = left_low
        factors_ref[1] = jnp.where(line >= lane, dot32(left_inverse, right_low, by_row), 0.0)

    return call(
        kernel,
        [image, rows_high, rows_low, mine, other, *quarters, left_rows],
        [shape(left_rows.shape), shape((block, width)), shape((2, block, block))],
        scratch=[pltpu.VMEM((block, count), f32), pltpu.VMEM((TILE, size), f32), pltpu.VMEM((TILE, size), f32)],
    )


def factor_left(gram, rows):
    def kernel(gram_ref, rows_ref, low_ref, inverse_ref, new_ref):
        low, inverse = eliminate(gram_ref[...])
        low_ref[...] = low
        inverse_ref[...] = inverse
        new_ref[...] = dot32(inverse, rows_ref[...], ((1,), (0,)))

    small = shape(gram.shape)
    return call(kernel, [gram, rows], [small, small, shape(rows.shape)])


def factor_right(gram, rows, left_low, left_inverse):
    def kernel(gram_ref, rows_ref, left_low_ref, left_inverse_ref, factors_ref, new_ref):
        low, inverse = eliminate(gram_ref[...])
        new_ref[...] = dot32(inverse, rows_ref[...], ((1,), (0,)))
        factors_ref[0] = left_low_ref[...]
        line = lax.broadcasted_iota(jnp.int32, low.shape, 0)
        lane = lax.broadcasted_iota(jnp.int32, low.shape, 1)
        factors_ref[1] = jnp.where(line >= lane, dot32(left_inverse_ref[...], low, ((1,), (0,))), 0.0)

    return call(kernel, [gram, rows, left_low, left_inverse], [shape((2, *gram.shape)), shape(rows.shape)])


def bases_split(bases):
    rows = jnp.concatenate(bases, 0)
    rows = jnp.pad(rows, ((0, padded(rows.shape[0]) - rows.shape[0]), (0, 0)))
    high, low = split(rows)
    return high, low, jnp.concatenate([high.T, low.T], 1)


def step(matrix, left_basis, right_basis, right_block, *, n_col, n_row):
    total = left_basis.shape[1] * n_col * n_row
    chunk, width = matrix.shape[0] // n_col, matrix.shape[1] // n_row
    tiled = n_col == 4 and n_row == 8 and width % 128 == 0 and chunk % 32 == 0
    row_swap = lambda values, bit: swap(values, "row", n_row, bit)
    col_swap = lambda values, bit: swap(values, "col", n_col, bit)

    def all_sum(values):
        values = values + row_swap(values, 1)
        values = exchange_sum(values, "row", n_row, 2)
        return exchange_sum(values, "col", n_col, 1)

    def split_sum(mine, theirs):
        mine = mine + row_swap(theirs, 1)
        mine = exchange_sum(mine, "row", n_row, 2)
        mine = exchange_sum(mine, "col", n_col, 1)
        return mine, row_swap(mine, 1)

    rounded = right_block.astype(bf16)
    prepared_rows = prepare if tiled else bases_split
    known = tiled and padded(right_basis.shape[0] + right_block.shape[0]) == 3 * TILE
    if tiled:
        lefts = {m: row_swap(rounded, m) for m in range(2, n_row, 2)}
        lefts[0], lefts[1] = rounded, row_swap(rounded, 1)
        chunk_2 = fetch(matrix, chunk, 2)
        chunk_2, *after = lax.optimization_barrier((chunk_2, *(lefts[m] for m in range(2, n_row, 2))))
        for m, values in zip(range(2, n_row, 2), after):
            lefts[m] = values
            lefts[m + 1] = row_swap(values, 1)
        order = sorted(lefts)
        piece_2, piece_3, chunk_3, chunk_1, whole = forward(
            [lefts[m] for m in order], order, {2: chunk_2}, matrix, chunk, [2, 3], [3, 1]
        )
        piece_1, chunk_0 = forward([whole], None, {1: chunk_1}, matrix, chunk, [1], [0])
        (piece_0,) = forward([whole], None, {0: chunk_0}, matrix, chunk, [0], [])
        pieces = [col_swap(piece_2, 2), col_swap(piece_3, 3)]
        pieces = [piece_0, col_swap(piece_1, 1)] + pieces
    else:
        whole = lax.all_gather(rounded, "row", axis=1, tiled=True)
        partial = dot16(whole, matrix, ((1,), (1,)))
        me = lax.axis_index("col")
        pieces = [lax.dynamic_slice_in_dim(partial, (me ^ j) * chunk, chunk, 1) for j in range(n_col)]
        pieces = [pieces[0]] + [col_swap(pieces[j].astype(CROSS), j) for j in range(1, n_col)]
    if tiled:
        pieces[0], left_basis = lax.optimization_barrier((pieces[0], left_basis))
    left_high, left_low, left_turned = prepared_rows([left_basis])
    image, mine, theirs = coefficients(pieces, left_turned, total)
    if known:
        image, right_basis, right_block = lax.optimization_barrier((image, right_basis, right_block))
        right_high, right_low, right_turned, kept, given = prepare([right_basis, right_block], total)
        given = row_swap(given, 1)
        quarters = quarter_sums(kept, given)
        quarters = [values if k == 0 else row_swap(values, 2 * k) for k, values in enumerate(quarters)]
    mine, other = split_sum(mine, theirs)
    projected, low, gram = project(image, left_high, left_low, mine, other, total)
    if tiled:
        lows = [col_swap(low, j) for j in range(1, n_col)]
        begun = backward_begin(lows[0], chunk_1, backward_begin(low, chunk_0))
        begun = backward_begin(lows[1], chunk_2, begun)
        if not known:
            begun, right_basis, right_block = lax.optimization_barrier((begun, right_basis, right_block))
        ready = (lows[2:], [chunk_3], begun)
        far = list(range(2, n_row, 2))
        (theirs,) = backward(*ready, [[m + 1 for m in far]], n_row)
        theirs = row_swap(theirs, 1)
        (mine,) = backward(*ready, [far], n_row)
        begun, *sent = lax.optimization_barrier((begun, *combine(mine, theirs)))
        pieces = [row_swap(values, m) for m, values in zip(far, sent)]
        theirs, mine = backward(*ready[:2], begun, [[1], [0]], n_row)
        pieces = [mine, row_swap(theirs, 1)] + pieces
        if known:
            gram_part = fold(quarters)
            gram_part = exchange_sum(gram_part, "col", n_col, 1)
            gram_other = row_swap(gram_part, 1)
            gram_part = pair(gram_part, gram_other)
    else:
        lows = [col_swap(low, j) for j in range(1, n_col)]
        me_col, me = lax.axis_index("col"), lax.axis_index("row")
        partial = sum(
            dot16(piece, lax.dynamic_slice_in_dim(matrix, (me_col ^ g) * chunk, chunk, 0), ((1,), (0,)))
            for g, piece in enumerate([low] + lows)
        )
        cut = [lax.dynamic_slice_in_dim(partial, (me ^ j) * width, width, 1) for j in range(n_row)]
        mine = jnp.stack(cut[0::2]) + row_swap(jnp.stack(cut[1::2]), 1)
        pieces = [mine[0]] + [row_swap(mine[m].astype(CROSS), 2 * m) for m in range(1, n_row // 2)]
    if known:
        coimage, mine, theirs = coefficients(pieces, right_turned, total, gram, True)
        mine, other = split_sum(mine, theirs)
        quarters = [gram_part] + [row_swap(gram_part, 2 * k) for k in range(1, 4)]
        return tuple(finish(coimage, right_high, right_low, mine, other, quarters, projected))
    right_high, right_low, right_turned = prepared_rows([right_basis, right_block])
    coimage, mine, theirs = coefficients(pieces, right_turned, total, gram)
    mine, other = split_sum(mine, theirs)
    coprojected, _, cogram, gram = project(coimage, right_high, right_low, mine, other, total)
    cogram = all_sum(cogram)
    factor, inverse, left_new = factor_left(gram, projected)
    factors, right_new = factor_right(cogram, coprojected, factor, inverse)
    return left_new, right_new, factors


def solution(mesh):
    in_specs = (
        P("row", "col"),
        P(None, ("row", "col")),
        P(None, ("col", "row")),
        P(None, ("col", "row")),
    )
    out_specs = (P(None, ("row", "col")), P(None, ("col", "row")), P())
    body = functools.partial(step, n_col=mesh.shape["col"], n_row=mesh.shape["row"])
    return jax.shard_map(body, mesh=mesh, in_specs=in_specs, out_specs=out_specs, check_vma=False)
```

profile of v0, /device:TPU:0, one launch (start us, length us, event | category | flops | bytes accessed | tf_op | source)
XLA Modules:
  0.0 112.0 jit_solution(9216814543976437914)
XLA Ops:
  0.6 0.9 convert_element_type.3.rest_0_
  1.6 4.0 %collective-permute-start.3 = (bf16[64,768]{1,0:T(8,128)(2,1)S(1)}, bf16[64,768]{1,0:T(8,128)(2,1)S(1)}, u32[]{:S(2)}, u32[]{:S(2)}) collective-permute-start(bf16[64,768]{1,0:T(8,128)(2,1)S(1)} %convert_element_type.3.rest_0_), channel_id=1, source_target_pairs={{0,6},{1,7},{2,4},{3,5},{4,2},{5,3},{6,0},{7,1},{8,14},{9,15},{10,... | collective-permute-start | bytes 294920 | tf_op jit(solution)/shard_map/ppermute | solution.py:56
  5.6 0.5 collective-permute-start.2
  6.2 3.8 %shard_map.67.rest_8_.a_ref = bf16[768,6144]{1,0:T(8,128)(2,1)S(1)} custom-call(bf16[3072,6144]{1,0:T(8,128)(2,1)} %rest_2_.1), custom_call_target="tpu_custom_call" | custom-call | tf_op jit(solution)/shard_map/pallas_call | solution.py:45
  10.8 0.5 collective-permute-start.5
  11.3 0.8 collective-permute-done.4.rest_3_
  12.6 7.1 %shard_map.68 = (bf16[64,768]{1,0:T(8,128)(2,1)S(1)}, bf16[64,768]{1,0:T(8,128)(2,1)S(1)}, bf16[768,6144]{1,0:T(8,128)(2,1)S(1)}, bf16[768,6144]{1,0:T(8,128)(2,1)S(1)}, bf16[64,6144]{1,0:T(8,128)(2,1)S(1)}) custom-call(bf16[64,768]{1,0:T(8,128)(2,1)S(1)} %convert_element_type.3.rest_0_, bf16[64,768]{1,0:T(8,128)(2,1)S(1)} %collective-permute-done.rest_1_, ...), custom_call_target="tpu_custom_call" | custom-call | tf_op jit(solution)/shard_map/pallas_call | solution.py:45
  19.7 2.7 %collective-permute-start.8 = (bf16[64,768]{1,0:T(8,128)(2,1)S(1)}, bf16[64,768]{1,0:T(8,128)(2,1)S(1)}, u32[]{:S(2)}, u32[]{:S(2)}) collective-permute-start(bf16[64,768]{1,0:T(8,128)(2,1)S(1)} %get-tuple-element.58), channel_id=1, source_target_pairs={{0,16},{8,24},{16,0},{24,8},{1,17},{9,25},{17,1},{25,9},{2,18},{10... | collective-permute-start | bytes 294920 | tf_op jit(solution)/shard_map/ppermute | solution.py:56
  22.4 1.3 %collective-permute-start.9 = (bf16[64,768]{1,0:T(8,128)(2,1)S(1)}, bf16[64,768]{1,0:T(8,128)(2,1)S(1)}, u32[]{:S(2)}, u32[]{:S(2)}) collective-permute-start(bf16[64,768]{1,0:T(8,128)(2,1)S(1)} %get-tuple-element.59), channel_id=1, source_target_pairs={{0,24},{8,16},{16,8},{24,0},{1,25},{9,17},{17,9},{25,1},{2,26},{10... | collective-permute-start | bytes 294920 | tf_op jit(solution)/shard_map/ppermute | solution.py:56
  23.7 3.8 %shard_map.69 = (bf16[64,768]{1,0:T(8,128)(2,1)S(1)}, bf16[768,6144]{1,0:T(8,128)(2,1)S(1)}) custom-call(bf16[64,6144]{1,0:T(8,128)(2,1)S(1)} %get-tuple-element.53.rest_0_, bf16[768,6144]{1,0:T(8,128)(2,1)S(1)} %get-tuple-element.54.rest_1_.a_ref, bf16[3072,6144]{1,0:T(8,128)(2,1)} %rest_2_.1), custom_call_target="tpu_custom_call" | custom-call | tf_op jit(solution)/shard_map/pallas_call | solution.py:45
  27.8 3.4 %shard_map.70.rest_0_ = f32[64,768]{1,0:T(8,128)S(1)} custom-call(bf16[64,6144]{1,0:T(8,128)(2,1)S(1)} %get-tuple-element.53.rest_0_, bf16[768,6144]{1,0:T(8,128)(2,1)S(1)} %get-tuple-element.55.rest_1_.a_ref), custom_call_target="tpu_custom_call" | custom-call | tf_op jit(solution)/shard_map/pallas_call | solution.py:45
  31.7 0.6 collective-permute-done.7.rest_1_
  32.8 1.2 %collective-permute-done.10 = f32[32,384]{1,0:T(8,128)S(1)} collective-permute-done((f32[32,384]{1,0:T(8,128)S(1)}, f32[32,384]{1,0:T(8,128)S(1)}, u32[]{:S(2)}, u32[]{:S(2)}) %collective-permute-start.10) | collective-permute-done | bytes 49184 | tf_op jit(solution)/shard_map/ppermute | solution.py:56
  34.1 2.4 %collective-permute-start.13 = (f32[32,384]{1,0:T(8,128)S(1)}, f32[32,384]{1,0:T(8,128)S(1)}, u32[]{:S(2)}, u32[]{:S(2)}) collective-permute-start(f32[32,384]{1,0:T(8,128)S(1)} %add.51), channel_id=1, source_target_pairs={{0,6},{1,7},{2,4},{3,5},{4,2},{5,3},{6,0},{7,1},{8,14},{9,15},{10,... | collective-permute-start | bytes 147464 | tf_op jit(solution)/shard_map/ppermute | solution.py:56
  36.5 0.6 collective-permute-start.12
  37.1 0.6 collective-permute-start.11
  37.6 1.5 %collective-permute-done.13 = f32[32,384]{1,0:T(8,128)S(1)} collective-permute-done((f32[32,384]{1,0:T(8,128)S(1)}, f32[32,384]{1,0:T(8,128)S(1)}, u32[]{:S(2)}, u32[]{:S(2)}) %collective-permute-start.13) | collective-permute-done | bytes 49184 | tf_op jit(solution)/shard_map/ppermute | solution.py:56
  39.1 1.5 %collective-permute-done.12 = f32[32,384]{1,0:T(8,128)S(1)} collective-permute-done((f32[32,384]{1,0:T(8,128)S(1)}, f32[32,384]{1,0:T(8,128)S(1)}, u32[]{:S(2)}, u32[]{:S(2)}) %collective-permute-start.12) | collective-permute-done | bytes 49184 | tf_op jit(solution)/shard_map/ppermute | solution.py:56
  40.6 0.6 collective-permute-done.11
  41.2 3.2 %collective-permute-start.16 = (f32[32,384]{1,0:T(8,128)S(1)}, f32[32,384]{1,0:T(8,128)S(1)}, u32[]{:S(2)}, u32[]{:S(2)}) collective-permute-start(f32[32,384]{1,0:T(8,128)S(1)} %add_add_fusion.4), channel_id=1, source_target_pairs={{0,24},{8,16},{16,8},{24,0},{1,25},{9,17},{17,9},{25,1},{2,26},{10... | collective-permute-start | bytes 147464 | tf_op jit(solution)/shard_map/ppermute | solution.py:56
  44.3 1.3 %collective-permute-start.14 = (f32[32,384]{1,0:T(8,128)S(1)}, f32[32,384]{1,0:T(8,128)S(1)}, u32[]{:S(2)}, u32[]{:S(2)}) collective-permute-start(f32[32,384]{1,0:T(8,128)S(1)} %add_add_fusion.4), channel_id=1, source_target_pairs={{0,8},{8,0},{16,24},{24,16},{1,9},{9,1},{17,25},{25,17},{2,10},{10... | collective-permute-start | bytes 147464 | tf_op jit(solution)/shard_map/ppermute | solution.py:56
  45.6 1.5 %collective-permute-done.16 = f32[32,384]{1,0:T(8,128)S(1)} collective-permute-done((f32[32,384]{1,0:T(8,128)S(1)}, f32[32,384]{1,0:T(8,128)S(1)}, u32[]{:S(2)}, u32[]{:S(2)}) %collective-permute-start.16) | collective-permute-done | bytes 49184 | tf_op jit(solution)/shard_map/ppermute | solution.py:56
  47.2 2.2 %collective-permute-done.15 = f32[32,384]{1,0:T(8,128)S(1)} collective-permute-done((f32[32,384]{1,0:T(8,128)S(1)}, f32[32,384]{1,0:T(8,128)S(1)}, u32[]{:S(2)}, u32[]{:S(2)}) %collective-permute-start.15) | collective-permute-done | bytes 49184 | tf_op jit(solution)/shard_map/ppermute | solution.py:56
  49.4 1.2 %collective-permute-done.17.other_ref = f32[32,384]{1,0:T(8,128)S(1)} collective-permute-done((f32[32,384]{1,0:T(8,128)S(1)}, f32[32,384]{1,0:T(8,128)S(1)}, u32[]{:S(2)}, u32[]{:S(2)}) %collective-permute-start.17) | collective-permute-done | bytes 49184 | tf_op jit(solution)/shard_map/ppermute | solution.py:56
  50.6 0.7 shard_map.73
  51.4 0.5 collective-permute-start.20
  51.8 2.0 %collective-permute-start.19 = (bf16[64,768]{1,0:T(8,128)(2,1)S(1)}, bf16[64,768]{1,0:T(8,128)(2,1)S(1)}, u32[]{:S(2)}, u32[]{:S(2)}) collective-permute-start(bf16[64,768]{1,0:T(8,128)(2,1)S(1)} %get-tuple-element.68.p_ref), channel_id=1, source_target_pairs={{0,16},{8,24},{16,0},{24,8},{1,17},{9,25},{17,1},{25,9},{2,18},{10... | collective-permute-start | bytes 294920 | tf_op jit(solution)/shard_map/ppermute | solution.py:56
  53.8 2.0 %collective-permute-start.18 = (bf16[64,768]{1,0:T(8,128)(2,1)S(1)}, bf16[64,768]{1,0:T(8,128)(2,1)S(1)}, u32[]{:S(2)}, u32[]{:S(2)}) collective-permute-start(bf16[64,768]{1,0:T(8,128)(2,1)S(1)} %get-tuple-element.68.p_ref), channel_id=1, source_target_pairs={{0,24},{8,16},{16,8},{24,0},{1,25},{9,17},{17,9},{25,1},{2,26},{10... | collective-permute-start | bytes 294920 | tf_op jit(solution)/shard_map/ppermute | solution.py:56
  55.8 1.7 %shard_map.74.rest_0_ = f32[64,6144]{1,0:T(8,128)S(1)} custom-call(bf16[64,768]{1,0:T(8,128)(2,1)S(1)} %get-tuple-element.68.p_ref, bf16[768,6144]{1,0:T(8,128)(2,1)S(1)} %get-tuple-element.55.rest_1_.a_ref), custom_call_target="tpu_custom_call" | custom-call | tf_op jit(solution)/shard_map/pallas_call | solution.py:45
  57.6 0.8 collective-permute-done.20.p_ref
  58.4 1.7 %shard_map.75.rest_0_ = f32[64,6144]{1,0:T(8,128)S(1)} custom-call(bf16[64,768]{1,0:T(8,128)(2,1)S(1)} %collective-permute-done.20.p_ref, bf16[768,6144]{1,0:T(8,128)(2,1)S(1)} %get-tuple-element.54.rest_1_.a_ref, f32[64,6144]{1,0:T(8,128)S(1)} %shard_map.74.rest_0_), custom_call_target="tpu_custom_call" | custom-call | tf_op jit(solution)/shard_map/pallas_call | solution.py:45
  60.2 1.7 %shard_map.76.rest_2_ = f32[64,6144]{1,0:T(8,128)S(1)} custom-call(bf16[64,768]{1,0:T(8,128)(2,1)S(1)} %collective-permute-done.19.p_ref, bf16[768,6144]{1,0:T(8,128)(2,1)S(1)} %shard_map.67.rest_8_.a_ref, f32[64,6144]{1,0:T(8,128)S(1)} %shard_map.75.rest_0_), custom_call_target="tpu_custom_call" | custom-call | tf_op jit(solution)/shard_map/pallas_call | solution.py:45
  62.1 0.8 shard_map.78
  63.0 0.8 shard_map.77.mine_ref
  63.8 1.2 %collective-permute-done.21.theirs_ref = f32[3,64,768]{2,1,0:T(8,128)S(1)} collective-permute-done((f32[3,64,768]{2,1,0:T(8,128)S(1)}, f32[3,64,768]{2,1,0:T(8,128)S(1)}, u32[]{:S(2)}, u32[]{:S(2)}) %collective-permute-start.21) | collective-permute-done | bytes 589856 | tf_op jit(solution)/shard_map/ppermute | solution.py:56
  65.0 0.6 shard_map.80
  65.8 1.5 %shard_map.81 = (bf16[384,768]{1,0:T(8,128)(2,1)S(1)}, bf16[384,768]{1,0:T(8,128)(2,1)S(1)}, bf16[768,768]{1,0:T(8,128)(2,1)S(1)}, f32[128,384]{1,0:T(8,128)S(1)}, f32[128,384]{1,0:T(8,128)S(1)}) custom-call(f32[320,768]{1,0:T(8,128)S(1)} %copy-done.1, f32[64,768]{1,0:T(8,128)S(1)} %copy-done.2), custom_call_target="tpu_custom_call" | custom-call | tf_op jit(solution)/shard_map/pallas_call | solution.py:45
  67.7 0.5 collective-permute-start.23
  68.3 1.5 %collective-permute-start.24 = (bf16[64,768]{1,0:T(8,128)(2,1)S(1)}, bf16[64,768]{1,0:T(8,128)(2,1)S(1)}, u32[]{:S(2)}, u32[]{:S(2)}) collective-permute-start(bf16[64,768]{1,0:T(8,128)(2,1)S(1)} %get-tuple-element.77), channel_id=1, source_target_pairs={{0,4},{1,5},{2,6},{3,7},{4,0},{5,1},{6,2},{7,3},{8,12},{9,13},{10,... | collective-permute-start | bytes 294920 | tf_op jit(solution)/shard_map/ppermute | solution.py:56
  69.8 1.4 %collective-permute-start.25 = (bf16[64,768]{1,0:T(8,128)(2,1)S(1)}, bf16[64,768]{1,0:T(8,128)(2,1)S(1)}, u32[]{:S(2)}, u32[]{:S(2)}) collective-permute-start(bf16[64,768]{1,0:T(8,128)(2,1)S(1)} %get-tuple-element.78), channel_id=1, source_target_pairs={{0,6},{1,7},{2,4},{3,5},{4,2},{5,3},{6,0},{7,1},{8,14},{9,15},{10,... | collective-permute-start | bytes 294920 | tf_op jit(solution)/shard_map/ppermute | solution.py:56
  71.2 2.0 %collective-permute-done.23.rest_2_ = bf16[64,768]{1,0:T(8,128)(2,1)S(1)} collective-permute-done((bf16[64,768]{1,0:T(8,128)(2,1)S(1)}, bf16[64,768]{1,0:T(8,128)(2,1)S(1)}, u32[]{:S(2)}, u32[]{:S(2)}) %collective-permute-start.23) | collective-permute-done | bytes 98336 | tf_op jit(solution)/shard_map/ppermute | solution.py:56
  73.2 0.8 collective-permute-done.24.rest_3_
  74.1 1.6 %collective-permute-done.25.rest_4_ = bf16[64,768]{1,0:T(8,128)(2,1)S(1)} collective-permute-done((bf16[64,768]{1,0:T(8,128)(2,1)S(1)}, bf16[64,768]{1,0:T(8,128)(2,1)S(1)}, u32[]{:S(2)}, u32[]{:S(2)}) %collective-permute-start.25) | collective-permute-done | bytes 98336 | tf_op jit(solution)/shard_map/ppermute | solution.py:56
  75.6 0.6 shard_map.82
  76.3 1.2 %collective-permute-start.35 = (f32[32,384]{1,0:T(8,128)S(1)}, f32[32,384]{1,0:T(8,128)S(1)}, u32[]{:S(2)}, u32[]{:S(2)}) collective-permute-start(f32[32,384]{1,0:T(8,128)S(1)} %get-tuple-element.91), channel_id=1, source_target_pairs={{0,2},{1,3},{2,0},{3,1},{4,6},{5,7},{6,4},{7,5},{8,10},{9,11},{10,... | collective-permute-start | bytes 147464 | tf_op jit(solution)/shard_map/ppermute | solution.py:56
  77.6 1.8 %collective-permute-start.29 = (f32[32,512]{1,0:T(8,128)S(1)}, f32[32,512]{1,0:T(8,128)S(1)}, u32[]{:S(2)}, u32[]{:S(2)}) collective-permute-start(f32[32,512]{1,0:T(8,128)S(1)} %add.58), channel_id=1, source_target_pairs={{0,6},{1,7},{2,4},{3,5},{4,2},{5,3},{6,0},{7,1},{8,14},{9,15},{10,... | collective-permute-start | bytes 196616 | tf_op jit(solution)/shard_map/ppermute | solution.py:56
  79.4 0.8 collective-permute-start.28
  80.2 0.9 collective-permute-start.27
  81.1 1.2 %collective-permute-start.36 = (f32[32,384]{1,0:T(8,128)S(1)}, f32[32,384]{1,0:T(8,128)S(1)}, u32[]{:S(2)}, u32[]{:S(2)}) collective-permute-start(f32[32,384]{1,0:T(8,128)S(1)} %get-tuple-element.92), channel_id=1, source_target_pairs={{0,4},{1,5},{2,6},{3,7},{4,0},{5,1},{6,2},{7,3},{8,12},{9,13},{10,... | collective-permute-start | bytes 147464 | tf_op jit(solution)/shard_map/ppermute | solution.py:56
  82.4 1.4 %collective-permute-start.37 = (f32[32,384]{1,0:T(8,128)S(1)}, f32[32,384]{1,0:T(8,128)S(1)}, u32[]{:S(2)}, u32[]{:S(2)}) collective-permute-start(f32[32,384]{1,0:T(8,128)S(1)} %get-tuple-element.93), channel_id=1, source_target_pairs={{0,6},{1,7},{2,4},{3,5},{4,2},{5,3},{6,0},{7,1},{8,14},{9,15},{10,... | collective-permute-start | bytes 147464 | tf_op jit(solution)/shard_map/ppermute | solution.py:56
  83.7 1.7 %collective-permute-done.36.c = f32[32,384]{1,0:T(8,128)S(1)} collective-permute-done((f32[32,384]{1,0:T(8,128)S(1)}, f32[32,384]{1,0:T(8,128)S(1)}, u32[]{:S(2)}, u32[]{:S(2)}) %collective-permute-start.36) | collective-permute-done | bytes 49184 | tf_op jit(solution)/shard_map/ppermute | solution.py:56
  85.4 1.9 %collective-permute-done.37.d = f32[32,384]{1,0:T(8,128)S(1)} collective-permute-done((f32[32,384]{1,0:T(8,128)S(1)}, f32[32,384]{1,0:T(8,128)S(1)}, u32[]{:S(2)}, u32[]{:S(2)}) %collective-permute-start.37) | collective-permute-done | bytes 49184 | tf_op jit(solution)/shard_map/ppermute | solution.py:56
  87.4 4.6 %collective-permute-start.40 = (f32[32,384]{1,0:T(8,128)S(1)}, f32[32,384]{1,0:T(8,128)S(1)}, u32[]{:S(2)}, u32[]{:S(2)}) collective-permute-start(f32[32,384]{1,0:T(8,128)S(1)} %shard_map.84), channel_id=1, source_target_pairs={{0,24},{8,16},{16,8},{24,0},{1,25},{9,17},{17,9},{25,1},{2,26},{10... | collective-permute-start | bytes 147464 | tf_op jit(solution)/shard_map/ppermute | solution.py:56
  92.0 0.6 collective-permute-start.38
  92.7 3.8 %collective-permute-start.32 = (f32[32,512]{1,0:T(8,128)S(1)}, f32[32,512]{1,0:T(8,128)S(1)}, u32[]{:S(2)}, u32[]{:S(2)}) collective-permute-start(f32[32,512]{1,0:T(8,128)S(1)} %add_add_fusion.1), channel_id=1, source_target_pairs={{0,24},{8,16},{16,8},{24,0},{1,25},{9,17},{17,9},{25,1},{2,26},{10... | collective-permute-start | bytes 196616 | tf_op jit(solution)/shard_map/ppermute | solution.py:56
  96.5 0.6 collective-permute-start.30
  97.1 1.1 collective-permute-done.39
  98.3 1.2 %collective-permute-done.41.other_ref = f32[32,384]{1,0:T(8,128)S(1)} collective-permute-done((f32[32,384]{1,0:T(8,128)S(1)}, f32[32,384]{1,0:T(8,128)S(1)}, u32[]{:S(2)}, u32[]{:S(2)}) %collective-permute-start.41) | collective-permute-done | bytes 49184 | tf_op jit(solution)/shard_map/ppermute | solution.py:56
  99.5 1.2 %collective-permute-start.44 = (f32[64,384]{1,0:T(8,128)S(1)}, f32[64,384]{1,0:T(8,128)S(1)}, u32[]{:S(2)}, u32[]{:S(2)}) collective-permute-start(f32[64,384]{1,0:T(8,128)S(1)} %shard_map.85.q0), channel_id=1, source_target_pairs={{0,6},{1,7},{2,4},{3,5},{4,2},{5,3},{6,0},{7,1},{8,14},{9,15},{10,... | collective-permute-start | bytes 294920 | tf_op jit(solution)/shard_map/ppermute | solution.py:56
  100.8 1.2 %collective-permute-start.43 = (f32[64,384]{1,0:T(8,128)S(1)}, f32[64,384]{1,0:T(8,128)S(1)}, u32[]{:S(2)}, u32[]{:S(2)}) collective-permute-start(f32[64,384]{1,0:T(8,128)S(1)} %shard_map.85.q0), channel_id=1, source_target_pairs={{0,4},{1,5},{2,6},{3,7},{4,0},{5,1},{6,2},{7,3},{8,12},{9,13},{10,... | collective-permute-start | bytes 294920 | tf_op jit(solution)/shard_map/ppermute | solution.py:56
  102.0 1.1 collective-permute-start.42
  103.2 3.0 %collective-permute-done.44.q3 = f32[64,384]{1,0:T(8,128)S(1)} collective-permute-done((f32[64,384]{1,0:T(8,128)S(1)}, f32[64,384]{1,0:T(8,128)S(1)}, u32[]{:S(2)}, u32[]{:S(2)}) %collective-permute-start.44) | collective-permute-done | bytes 98336 | tf_op jit(solution)/shard_map/ppermute | solution.py:56
  106.2 1.3 %collective-permute-done.43.q2 = f32[64,384]{1,0:T(8,128)S(1)} collective-permute-done((f32[64,384]{1,0:T(8,128)S(1)}, f32[64,384]{1,0:T(8,128)S(1)}, u32[]{:S(2)}, u32[]{:S(2)}) %collective-permute-start.43) | collective-permute-done | bytes 98336 | tf_op jit(solution)/shard_map/ppermute | solution.py:56
  107.5 4.5 %shard_map.86 = (f32[64,768]{1,0:T(8,128)}, f32[64,768]{1,0:T(8,128)}, f32[2,64,64]{2,1,0:T(8,128)}) custom-call(f32[64,768]{1,0:T(8,128)S(1)} %get-tuple-element.83.image_ref, bf16[384,768]{1,0:T(8,128)(2,1)S(1)} %get-tuple-element.84.high_ref, bf16[384,768]{1,0:T(8,128)(2,1)S(1)} %get-tuple-element.85.low_ref, f32[32,512]{1,0:T(8,128)S(1)} %add_add_fusion.mine_ref, ...), custom_call_target="tpu_custom_call" | custom-call | tf_op jit(solution)/shard_map/pallas_call | solution.py:45
  (60 shorter events, 4.1 us)
Async XLA Ops:
  1.6 8.4 %collective-permute-start.3 = (bf16[64,768]{1,0:T(8,128)(2,1)S(1)}, bf16[64,768]{1,0:T(8,128)(2,1)S(1)}, u32[]{:S(2)}, u32[]{:S(2)}) collective-permute-start(bf16[64,768]{1,0:T(8,128)(2,1)S(1)} %convert_element_type.3.rest_0_), channel_id=1, source_target_pairs={{0,6},{1,7},{2,4},{3,5},{4,2},{5,3},{6,0},{7,1},{8,14},{9,15},{10,... | collective-permute-start | bytes 294920 | tf_op jit(solution)/shard_map/ppermute | solution.py:56
  5.6 4.9 %collective-permute-start.2 = (bf16[64,768]{1,0:T(8,128)(2,1)S(1)}, bf16[64,768]{1,0:T(8,128)(2,1)S(1)}, u32[]{:S(2)}, u32[]{:S(2)}) collective-permute-start(bf16[64,768]{1,0:T(8,128)(2,1)S(1)} %convert_element_type.3.rest_0_), channel_id=1, source_target_pairs={{0,4},{1,5},{2,6},{3,7},{4,0},{5,1},{6,2},{7,3},{8,12},{9,13},{10,... | collective-permute-start | bytes 294920 | tf_op jit(solution)/shard_map/ppermute | solution.py:56
  6.1 4.7 %collective-permute-start.1 = (bf16[64,768]{1,0:T(8,128)(2,1)S(1)}, bf16[64,768]{1,0:T(8,128)(2,1)S(1)}, u32[]{:S(2)}, u32[]{:S(2)}) collective-permute-start(bf16[64,768]{1,0:T(8,128)(2,1)S(1)} %convert_element_type.3.rest_0_), channel_id=1, source_target_pairs={{0,2},{1,3},{2,0},{3,1},{4,6},{5,7},{6,4},{7,5},{8,10},{9,11},{10,... | collective-permute-start | bytes 294920 | tf_op jit(solution)/shard_map/ppermute | solution.py:56
  6.2 5.1 %collective-permute-start = (bf16[64,768]{1,0:T(8,128)(2,1)S(1)}, bf16[64,768]{1,0:T(8,128)(2,1)S(1)}, u32[]{:S(2)}, u32[]{:S(2)}) collective-permute-start(bf16[64,768]{1,0:T(8,128)(2,1)S(1)} %convert_element_type.3.rest_0_), channel_id=1, source_target_pairs={{0,1},{1,0},{2,3},{3,2},{4,5},{5,4},{6,7},{7,6},{8,9},{9,8},{10,11... | collective-permute-start | bytes 294920 | tf_op jit(solution)/shard_map/ppermute | solution.py:56
  10.8 1.3 %collective-permute-start.4 = (bf16[64,768]{1,0:T(8,128)(2,1)S(1)}, bf16[64,768]{1,0:T(8,128)(2,1)S(1)}, u32[]{:S(2)}, u32[]{:S(2)}) collective-permute-start(bf16[64,768]{1,0:T(8,128)(2,1)S(1)} %collective-permute-done.1.rest_2_), channel_id=1, source_target_pairs={{0,1},{1,0},{2,3},{3,2},{4,5},{5,4},{6,7},{7,6},{8,9},{9,8},{10,11... | collective-permute-start | bytes 294920 | tf_op jit(solution)/shard_map/ppermute | solution.py:56
  10.8 1.5 %collective-permute-start.5 = (bf16[64,768]{1,0:T(8,128)(2,1)S(1)}, bf16[64,768]{1,0:T(8,128)(2,1)S(1)}, u32[]{:S(2)}, u32[]{:S(2)}) collective-permute-start(bf16[64,768]{1,0:T(8,128)(2,1)S(1)} %collective-permute-done.2.rest_4_), channel_id=1, source_target_pairs={{0,1},{1,0},{2,3},{3,2},{4,5},{5,4},{6,7},{7,6},{8,9},{9,8},{10,11... | collective-permute-start | bytes 294920 | tf_op jit(solution)/shard_map/ppermute | solution.py:56
  11.3 1.3 %collective-permute-start.6 = (bf16[64,768]{1,0:T(8,128)(2,1)S(1)}, bf16[64,768]{1,0:T(8,128)(2,1)S(1)}, u32[]{:S(2)}, u32[]{:S(2)}) collective-permute-start(bf16[64,768]{1,0:T(8,128)(2,1)S(1)} %collective-permute-done.3.rest_6_), channel_id=1, source_target_pairs={{0,1},{1,0},{2,3},{3,2},{4,5},{5,4},{6,7},{7,6},{8,9},{9,8},{10,11... | collective-permute-start | bytes 294920 | tf_op jit(solution)/shard_map/ppermute | solution.py:56
  19.7 12.0 %collective-permute-start.8 = (bf16[64,768]{1,0:T(8,128)(2,1)S(1)}, bf16[64,768]{1,0:T(8,128)(2,1)S(1)}, u32[]{:S(2)}, u32[]{:S(2)}) collective-permute-start(bf16[64,768]{1,0:T(8,128)(2,1)S(1)} %get-tuple-element.58), channel_id=1, source_target_pairs={{0,16},{8,24},{16,0},{24,8},{1,17},{9,25},{17,1},{25,9},{2,18},{10... | collective-permute-start | bytes 294920 | tf_op jit(solution)/shard_map/ppermute | solution.py:56
  22.4 9.3 %collective-permute-start.9 = (bf16[64,768]{1,0:T(8,128)(2,1)S(1)}, bf16[64,768]{1,0:T(8,128)(2,1)S(1)}, u32[]{:S(2)}, u32[]{:S(2)}) collective-permute-start(bf16[64,768]{1,0:T(8,128)(2,1)S(1)} %get-tuple-element.59), channel_id=1, source_target_pairs={{0,24},{8,16},{16,8},{24,0},{1,25},{9,17},{17,9},{25,1},{2,26},{10... | collective-permute-start | bytes 294920 | tf_op jit(solution)/shard_map/ppermute | solution.py:56
  27.5 3.7 %copy-start = (f32[320,768]{1,0:T(8,128)S(1)}, f32[320,768]{1,0:T(8,128)}, u32[]{:S(2)}) copy-start(f32[320,768]{1,0:T(8,128)} %rest_0_) | copy-start | bytes 2949124
  27.5 4.8 %collective-permute-start.7 = (bf16[64,768]{1,0:T(8,128)(2,1)S(1)}, bf16[64,768]{1,0:T(8,128)(2,1)S(1)}, u32[]{:S(2)}, u32[]{:S(2)}) collective-permute-start(bf16[64,768]{1,0:T(8,128)(2,1)S(1)} %get-tuple-element.57), channel_id=1, source_target_pairs={{0,8},{8,0},{16,24},{24,16},{1,9},{9,1},{17,25},{25,17},{2,10},{10... | collective-permute-start | bytes 294920 | tf_op jit(solution)/shard_map/ppermute | solution.py:56
  32.7 1.3 %collective-permute-start.10 = (f32[32,384]{1,0:T(8,128)S(1)}, f32[32,384]{1,0:T(8,128)S(1)}, u32[]{:S(2)}, u32[]{:S(2)}) collective-permute-start(f32[32,384]{1,0:T(8,128)S(1)} %get-tuple-element.67), channel_id=1, source_target_pairs={{0,1},{1,0},{2,3},{3,2},{4,5},{5,4},{6,7},{7,6},{8,9},{9,8},{10,11... | collective-permute-start | bytes 147464 | tf_op jit(solution)/shard_map/ppermute | solution.py:56
  34.1 5.1 %collective-permute-start.13 = (f32[32,384]{1,0:T(8,128)S(1)}, f32[32,384]{1,0:T(8,128)S(1)}, u32[]{:S(2)}, u32[]{:S(2)}) collective-permute-start(f32[32,384]{1,0:T(8,128)S(1)} %add.51), channel_id=1, source_target_pairs={{0,6},{1,7},{2,4},{3,5},{4,2},{5,3},{6,0},{7,1},{8,14},{9,15},{10,... | collective-permute-start | bytes 147464 | tf_op jit(solution)/shard_map/ppermute | solution.py:56
  36.5 4.1 %collective-permute-start.12 = (f32[32,384]{1,0:T(8,128)S(1)}, f32[32,384]{1,0:T(8,128)S(1)}, u32[]{:S(2)}, u32[]{:S(2)}) collective-permute-start(f32[32,384]{1,0:T(8,128)S(1)} %add.51), channel_id=1, source_target_pairs={{0,4},{1,5},{2,6},{3,7},{4,0},{5,1},{6,2},{7,3},{8,12},{9,13},{10,... | collective-permute-start | bytes 147464 | tf_op jit(solution)/shard_map/ppermute | solution.py:56
  37.1 4.1 %collective-permute-start.11 = (f32[32,384]{1,0:T(8,128)S(1)}, f32[32,384]{1,0:T(8,128)S(1)}, u32[]{:S(2)}, u32[]{:S(2)}) collective-permute-start(f32[32,384]{1,0:T(8,128)S(1)} %add.51), channel_id=1, source_target_pairs={{0,2},{1,3},{2,0},{3,1},{4,6},{5,7},{6,4},{7,5},{8,10},{9,11},{10,... | collective-permute-start | bytes 147464 | tf_op jit(solution)/shard_map/ppermute | solution.py:56
  41.2 6.0 %collective-permute-start.16 = (f32[32,384]{1,0:T(8,128)S(1)}, f32[32,384]{1,0:T(8,128)S(1)}, u32[]{:S(2)}, u32[]{:S(2)}) collective-permute-start(f32[32,384]{1,0:T(8,128)S(1)} %add_add_fusion.4), channel_id=1, source_target_pairs={{0,24},{8,16},{16,8},{24,0},{1,25},{9,17},{17,9},{25,1},{2,26},{10... | collective-permute-start | bytes 147464 | tf_op jit(solution)/shard_map/ppermute | solution.py:56
  44.3 5.0 %collective-permute-start.15 = (f32[32,384]{1,0:T(8,128)S(1)}, f32[32,384]{1,0:T(8,128)S(1)}, u32[]{:S(2)}, u32[]{:S(2)}) collective-permute-start(f32[32,384]{1,0:T(8,128)S(1)} %add_add_fusion.4), channel_id=1, source_target_pairs={{0,16},{8,24},{16,0},{24,8},{1,17},{9,25},{17,1},{25,9},{2,18},{10... | collective-permute-start | bytes 147464 | tf_op jit(solution)/shard_map/ppermute | solution.py:56
  44.3 5.0 %collective-permute-start.14 = (f32[32,384]{1,0:T(8,128)S(1)}, f32[32,384]{1,0:T(8,128)S(1)}, u32[]{:S(2)}, u32[]{:S(2)}) collective-permute-start(f32[32,384]{1,0:T(8,128)S(1)} %add_add_fusion.4), channel_id=1, source_target_pairs={{0,8},{8,0},{16,24},{24,16},{1,9},{9,1},{17,25},{25,17},{2,10},{10... | collective-permute-start | bytes 147464 | tf_op jit(solution)/shard_map/ppermute | solution.py:56
  49.3 1.3 %collective-permute-start.17 = (f32[32,384]{1,0:T(8,128)S(1)}, f32[32,384]{1,0:T(8,128)S(1)}, u32[]{:S(2)}, u32[]{:S(2)}) collective-permute-start(f32[32,384]{1,0:T(8,128)S(1)} %add_add_fusion.3.mine_ref), channel_id=1, source_target_pairs={{0,1},{1,0},{2,3},{3,2},{4,5},{5,4},{6,7},{7,6},{8,9},{9,8},{10,11... | collective-permute-start | bytes 147464 | tf_op jit(solution)/shard_map/ppermute | solution.py:56
  51.4 7.0 %collective-permute-start.20 = (bf16[64,768]{1,0:T(8,128)(2,1)S(1)}, bf16[64,768]{1,0:T(8,128)(2,1)S(1)}, u32[]{:S(2)}, u32[]{:S(2)}) collective-permute-start(bf16[64,768]{1,0:T(8,128)(2,1)S(1)} %get-tuple-element.68.p_ref), channel_id=1, source_target_pairs={{0,8},{8,0},{16,24},{24,16},{1,9},{9,1},{17,25},{25,17},{2,10},{10... | collective-permute-start | bytes 294920 | tf_op jit(solution)/shard_map/ppermute | solution.py:56
  51.8 8.3 %collective-permute-start.19 = (bf16[64,768]{1,0:T(8,128)(2,1)S(1)}, bf16[64,768]{1,0:T(8,128)(2,1)S(1)}, u32[]{:S(2)}, u32[]{:S(2)}) collective-permute-start(bf16[64,768]{1,0:T(8,128)(2,1)S(1)} %get-tuple-element.68.p_ref), channel_id=1, source_target_pairs={{0,16},{8,24},{16,0},{24,8},{1,17},{9,25},{17,1},{25,9},{2,18},{10... | collective-permute-start | bytes 294920 | tf_op jit(solution)/shard_map/ppermute | solution.py:56
  53.8 8.3 %collective-permute-start.18 = (bf16[64,768]{1,0:T(8,128)(2,1)S(1)}, bf16[64,768]{1,0:T(8,128)(2,1)S(1)}, u32[]{:S(2)}, u32[]{:S(2)}) collective-permute-start(bf16[64,768]{1,0:T(8,128)(2,1)S(1)} %get-tuple-element.68.p_ref), channel_id=1, source_target_pairs={{0,24},{8,16},{16,8},{24,0},{1,25},{9,17},{17,9},{25,1},{2,26},{10... | collective-permute-start | bytes 294920 | tf_op jit(solution)/shard_map/ppermute | solution.py:56
  62.9 2.9 %copy-start.1 = (f32[320,768]{1,0:T(8,128)S(1)}, f32[320,768]{1,0:T(8,128)}, u32[]{:S(2)}) copy-start(f32[320,768]{1,0:T(8,128)} %rest_0_.1) | copy-start | bytes 2949124
  62.9 2.9 %copy-start.2 = (f32[64,768]{1,0:T(8,128)S(1)}, f32[64,768]{1,0:T(8,128)}, u32[]{:S(2)}) copy-start(f32[64,768]{1,0:T(8,128)} %rest_1_) | copy-start | bytes 589828
  62.9 2.1 %collective-permute-start.21 = (f32[3,64,768]{2,1,0:T(8,128)S(1)}, f32[3,64,768]{2,1,0:T(8,128)S(1)}, u32[]{:S(2)}, u32[]{:S(2)}) collective-permute-start(f32[3,64,768]{2,1,0:T(8,128)S(1)} %shard_map.78), channel_id=1, source_target_pairs={{0,1},{1,0},{2,3},{3,2},{4,5},{5,4},{6,7},{7,6},{8,9},{9,8},{10,11... | collective-permute-start | bytes 1769480 | tf_op jit(solution)/shard_map/ppermute | solution.py:56
  65.6 10.1 %collective-permute-start.22 = (f32[1,64,768]{2,1,0:T(8,128)S(1)}, f32[1,64,768]{2,1,0:T(8,128)S(1)}, u32[]{:S(2)}, u32[]{:S(2)}) collective-permute-start(f32[1,64,768]{2,1,0:T(8,128)S(1)} %get-tuple-element.75), channel_id=1, source_target_pairs={{0,1},{1,0},{2,3},{3,2},{4,5},{5,4},{6,7},{7,6},{8,9},{9,8},{10,11... | collective-permute-start | bytes 589832 | tf_op jit(solution)/shard_map/ppermute | solution.py:56
  67.3 9.0 %collective-permute-start.34 = (f32[128,384]{1,0:T(8,128)S(1)}, f32[128,384]{1,0:T(8,128)S(1)}, u32[]{:S(2)}, u32[]{:S(2)}) collective-permute-start(f32[128,384]{1,0:T(8,128)S(1)} %get-tuple-element.89), channel_id=1, source_target_pairs={{0,1},{1,0},{2,3},{3,2},{4,5},{5,4},{6,7},{7,6},{8,9},{9,8},{10,11... | collective-permute-start | bytes 589832 | tf_op jit(solution)/shard_map/ppermute | solution.py:56
  67.7 5.5 %collective-permute-start.23 = (bf16[64,768]{1,0:T(8,128)(2,1)S(1)}, bf16[64,768]{1,0:T(8,128)(2,1)S(1)}, u32[]{:S(2)}, u32[]{:S(2)}) collective-permute-start(bf16[64,768]{1,0:T(8,128)(2,1)S(1)} %get-tuple-element.76), channel_id=1, source_target_pairs={{0,2},{1,3},{2,0},{3,1},{4,6},{5,7},{6,4},{7,5},{8,10},{9,11},{10,... | collective-permute-start | bytes 294920 | tf_op jit(solution)/shard_map/ppermute | solution.py:56
  68.3 5.8 %collective-permute-start.24 = (bf16[64,768]{1,0:T(8,128)(2,1)S(1)}, bf16[64,768]{1,0:T(8,128)(2,1)S(1)}, u32[]{:S(2)}, u32[]{:S(2)}) collective-permute-start(bf16[64,768]{1,0:T(8,128)(2,1)S(1)} %get-tuple-element.77), channel_id=1, source_target_pairs={{0,4},{1,5},{2,6},{3,7},{4,0},{5,1},{6,2},{7,3},{8,12},{9,13},{10,... | collective-permute-start | bytes 294920 | tf_op jit(solution)/shard_map/ppermute | solution.py:56
  69.8 5.8 %collective-permute-start.25 = (bf16[64,768]{1,0:T(8,128)(2,1)S(1)}, bf16[64,768]{1,0:T(8,128)(2,1)S(1)}, u32[]{:S(2)}, u32[]{:S(2)}) collective-permute-start(bf16[64,768]{1,0:T(8,128)(2,1)S(1)} %get-tuple-element.78), channel_id=1, source_target_pairs={{0,6},{1,7},{2,4},{3,5},{4,2},{5,3},{6,0},{7,1},{8,14},{9,15},{10,... | collective-permute-start | bytes 294920 | tf_op jit(solution)/shard_map/ppermute | solution.py:56
  76.2 1.4 %collective-permute-start.26 = (f32[32,512]{1,0:T(8,128)S(1)}, f32[32,512]{1,0:T(8,128)S(1)}, u32[]{:S(2)}, u32[]{:S(2)}) collective-permute-start(f32[32,512]{1,0:T(8,128)S(1)} %get-tuple-element.87), channel_id=1, source_target_pairs={{0,1},{1,0},{2,3},{3,2},{4,5},{5,4},{6,7},{7,6},{8,9},{9,8},{10,11... | collective-permute-start | bytes 196616 | tf_op jit(solution)/shard_map/ppermute | solution.py:56
  76.3 6.0 %collective-permute-start.35 = (f32[32,384]{1,0:T(8,128)S(1)}, f32[32,384]{1,0:T(8,128)S(1)}, u32[]{:S(2)}, u32[]{:S(2)}) collective-permute-start(f32[32,384]{1,0:T(8,128)S(1)} %get-tuple-element.91), channel_id=1, source_target_pairs={{0,2},{1,3},{2,0},{3,1},{4,6},{5,7},{6,4},{7,5},{8,10},{9,11},{10,... | collective-permute-start | bytes 147464 | tf_op jit(solution)/shard_map/ppermute | solution.py:56
  77.6 14.4 %collective-permute-start.29 = (f32[32,512]{1,0:T(8,128)S(1)}, f32[32,512]{1,0:T(8,128)S(1)}, u32[]{:S(2)}, u32[]{:S(2)}) collective-permute-start(f32[32,512]{1,0:T(8,128)S(1)} %add.58), channel_id=1, source_target_pairs={{0,6},{1,7},{2,4},{3,5},{4,2},{5,3},{6,0},{7,1},{8,14},{9,15},{10,... | collective-permute-start | bytes 196616 | tf_op jit(solution)/shard_map/ppermute | solution.py:56
  79.4 13.2 %collective-permute-start.28 = (f32[32,512]{1,0:T(8,128)S(1)}, f32[32,512]{1,0:T(8,128)S(1)}, u32[]{:S(2)}, u32[]{:S(2)}) collective-permute-start(f32[32,512]{1,0:T(8,128)S(1)} %add.58), channel_id=1, source_target_pairs={{0,4},{1,5},{2,6},{3,7},{4,0},{5,1},{6,2},{7,3},{8,12},{9,13},{10,... | collective-permute-start | bytes 196616 | tf_op jit(solution)/shard_map/ppermute | solution.py:56
  80.2 12.4 %collective-permute-start.27 = (f32[32,512]{1,0:T(8,128)S(1)}, f32[32,512]{1,0:T(8,128)S(1)}, u32[]{:S(2)}, u32[]{:S(2)}) collective-permute-start(f32[32,512]{1,0:T(8,128)S(1)} %add.58), channel_id=1, source_target_pairs={{0,2},{1,3},{2,0},{3,1},{4,6},{5,7},{6,4},{7,5},{8,10},{9,11},{10,... | collective-permute-start | bytes 196616 | tf_op jit(solution)/shard_map/ppermute | solution.py:56
  81.1 4.3 %collective-permute-start.36 = (f32[32,384]{1,0:T(8,128)S(1)}, f32[32,384]{1,0:T(8,128)S(1)}, u32[]{:S(2)}, u32[]{:S(2)}) collective-permute-start(f32[32,384]{1,0:T(8,128)S(1)} %get-tuple-element.92), channel_id=1, source_target_pairs={{0,4},{1,5},{2,6},{3,7},{4,0},{5,1},{6,2},{7,3},{8,12},{9,13},{10,... | collective-permute-start | bytes 147464 | tf_op jit(solution)/shard_map/ppermute | solution.py:56
  82.4 5.0 %collective-permute-start.37 = (f32[32,384]{1,0:T(8,128)S(1)}, f32[32,384]{1,0:T(8,128)S(1)}, u32[]{:S(2)}, u32[]{:S(2)}) collective-permute-start(f32[32,384]{1,0:T(8,128)S(1)} %get-tuple-element.93), channel_id=1, source_target_pairs={{0,6},{1,7},{2,4},{3,5},{4,2},{5,3},{6,0},{7,1},{8,14},{9,15},{10,... | collective-permute-start | bytes 147464 | tf_op jit(solution)/shard_map/ppermute | solution.py:56
  87.4 9.1 %collective-permute-start.40 = (f32[32,384]{1,0:T(8,128)S(1)}, f32[32,384]{1,0:T(8,128)S(1)}, u32[]{:S(2)}, u32[]{:S(2)}) collective-permute-start(f32[32,384]{1,0:T(8,128)S(1)} %shard_map.84), channel_id=1, source_target_pairs={{0,24},{8,16},{16,8},{24,0},{1,25},{9,17},{17,9},{25,1},{2,26},{10... | collective-permute-start | bytes 147464 | tf_op jit(solution)/shard_map/ppermute | solution.py:56
  92.0 6.2 %collective-permute-start.39 = (f32[32,384]{1,0:T(8,128)S(1)}, f32[32,384]{1,0:T(8,128)S(1)}, u32[]{:S(2)}, u32[]{:S(2)}) collective-permute-start(f32[32,384]{1,0:T(8,128)S(1)} %shard_map.84), channel_id=1, source_target_pairs={{0,16},{8,24},{16,0},{24,8},{1,17},{9,25},{17,1},{25,9},{2,18},{10... | collective-permute-start | bytes 147464 | tf_op jit(solution)/shard_map/ppermute | solution.py:56
  92.0 6.2 %collective-permute-start.38 = (f32[32,384]{1,0:T(8,128)S(1)}, f32[32,384]{1,0:T(8,128)S(1)}, u32[]{:S(2)}, u32[]{:S(2)}) collective-permute-start(f32[32,384]{1,0:T(8,128)S(1)} %shard_map.84), channel_id=1, source_target_pairs={{0,8},{8,0},{16,24},{24,16},{1,9},{9,1},{17,25},{25,17},{2,10},{10... | collective-permute-start | bytes 147464 | tf_op jit(solution)/shard_map/ppermute | solution.py:56
  92.7 9.4 %collective-permute-start.32 = (f32[32,512]{1,0:T(8,128)S(1)}, f32[32,512]{1,0:T(8,128)S(1)}, u32[]{:S(2)}, u32[]{:S(2)}) collective-permute-start(f32[32,512]{1,0:T(8,128)S(1)} %add_add_fusion.1), channel_id=1, source_target_pairs={{0,24},{8,16},{16,8},{24,0},{1,25},{9,17},{17,9},{25,1},{2,26},{10... | collective-permute-start | bytes 196616 | tf_op jit(solution)/shard_map/ppermute | solution.py:56
  96.5 6.6 %collective-permute-start.31 = (f32[32,512]{1,0:T(8,128)S(1)}, f32[32,512]{1,0:T(8,128)S(1)}, u32[]{:S(2)}, u32[]{:S(2)}) collective-permute-start(f32[32,512]{1,0:T(8,128)S(1)} %add_add_fusion.1), channel_id=1, source_target_pairs={{0,16},{8,24},{16,0},{24,8},{1,17},{9,25},{17,1},{25,9},{2,18},{10... | collective-permute-start | bytes 196616 | tf_op jit(solution)/shard_map/ppermute | solution.py:56
  96.5 6.6 %collective-permute-start.30 = (f32[32,512]{1,0:T(8,128)S(1)}, f32[32,512]{1,0:T(8,128)S(1)}, u32[]{:S(2)}, u32[]{:S(2)}) collective-permute-start(f32[32,512]{1,0:T(8,128)S(1)} %add_add_fusion.1), channel_id=1, source_target_pairs={{0,8},{8,0},{16,24},{24,16},{1,9},{9,1},{17,25},{25,17},{2,10},{10... | collective-permute-start | bytes 196616 | tf_op jit(solution)/shard_map/ppermute | solution.py:56
  98.2 1.3 %collective-permute-start.41 = (f32[32,384]{1,0:T(8,128)S(1)}, f32[32,384]{1,0:T(8,128)S(1)}, u32[]{:S(2)}, u32[]{:S(2)}) collective-permute-start(f32[32,384]{1,0:T(8,128)S(1)} %add_add_fusion.2.own_ref), channel_id=1, source_target_pairs={{0,1},{1,0},{2,3},{3,2},{4,5},{5,4},{6,7},{7,6},{8,9},{9,8},{10,11... | collective-permute-start | bytes 147464 | tf_op jit(solution)/shard_map/ppermute | solution.py:56
  99.5 6.7 %collective-permute-start.44 = (f32[64,384]{1,0:T(8,128)S(1)}, f32[64,384]{1,0:T(8,128)S(1)}, u32[]{:S(2)}, u32[]{:S(2)}) collective-permute-start(f32[64,384]{1,0:T(8,128)S(1)} %shard_map.85.q0), channel_id=1, source_target_pairs={{0,6},{1,7},{2,4},{3,5},{4,2},{5,3},{6,0},{7,1},{8,14},{9,15},{10,... | collective-permute-start | bytes 294920 | tf_op jit(solution)/shard_map/ppermute | solution.py:56
  100.8 6.7 %collective-permute-start.43 = (f32[64,384]{1,0:T(8,128)S(1)}, f32[64,384]{1,0:T(8,128)S(1)}, u32[]{:S(2)}, u32[]{:S(2)}) collective-permute-start(f32[64,384]{1,0:T(8,128)S(1)} %shard_map.85.q0), channel_id=1, source_target_pairs={{0,4},{1,5},{2,6},{3,7},{4,0},{5,1},{6,2},{7,3},{8,12},{9,13},{10,... | collective-permute-start | bytes 294920 | tf_op jit(solution)/shard_map/ppermute | solution.py:56
  102.0 5.5 %collective-permute-start.42 = (f32[64,384]{1,0:T(8,128)S(1)}, f32[64,384]{1,0:T(8,128)S(1)}, u32[]{:S(2)}, u32[]{:S(2)}) collective-permute-start(f32[64,384]{1,0:T(8,128)S(1)} %shard_map.85.q0), channel_id=1, source_target_pairs={{0,2},{1,3},{2,0},{3,1},{4,6},{5,7},{6,4},{7,5},{8,10},{9,11},{10,... | collective-permute-start | bytes 294920 | tf_op jit(solution)/shard_map/ppermute | solution.py:56
  103.1 4.3 %collective-permute-start.33 = (f32[32,512]{1,0:T(8,128)S(1)}, f32[32,512]{1,0:T(8,128)S(1)}, u32[]{:S(2)}, u32[]{:S(2)}) collective-permute-start(f32[32,512]{1,0:T(8,128)S(1)} %add_add_fusion.mine_ref), channel_id=1, source_target_pairs={{0,1},{1,0},{2,3},{3,2},{4,5},{5,4},{6,7},{7,6},{8,9},{9,8},{10,11... | collective-permute-start | bytes 196616 | tf_op jit(solution)/shard_map/ppermute | solution.py:56
where the time goes:
time: 112 us
  starting transfers between devices  47.1 us (42%)
  Pallas kernels  33.7 us (30%)
  waiting for transfers between devices  29.2 us (26%)
    ppermute x45, starting transfers between devices, swap(): return lax.ppermute(values, axis, [(i, i ^ bit) for i in range(size)])  47.1 us
    pallas_call x20, Pallas kernels, call(): pl.pallas_call(kernel, in_specs=specs or [VMEM] * len(inputs), out_specs=...  33.7 us
    ppermute x45, waiting for transfers between devices, swap(): return lax.ppermute(values, axis, [(i, i ^ bit) for i in range(size)])  29.2 us
  transfers between devices with their start and end apart: 45, of which 25 were waited for; matrix products, arithmetic and copies ran while one was open for 0% of the time, Pallas kernels for 17%

commit v1 on v0

--- a/solution.py
+++ b/solution.py
@@ -27,6 +27,11 @@
 def split(values):
     high = values.astype(bf16)
     return high, (values - high.astype(f32)).astype(bf16)
+
+
+def dot_split(first, second, dims):
+    (a, b), (c, d) = split(first), split(second)
+    return dot16(a, c, dims) + (dot16(a, d, dims) + dot16(b, c, dims))
 
 
 def limit(mebibytes):
@@ -396,12 +401,12 @@
         coefs = held[:, :size]
         first, second, third = (coefs[:, n * TILE : (n + 1) * TILE] for n in range(3))
         by_row = ((1,), (0,))
-        last = dot32(third, far[...], by_row)
-        middle = dot32(second, near[:, TILE:], by_row)
-        start = 0.5 * dot32(first, near[:, :TILE], by_row) + middle[:, :TILE] + last[:, :TILE]
+        last = dot_split(third, far[...], by_row)
+        middle = dot_split(second, near[:, TILE:], by_row)
+        start = 0.5 * dot_split(first, near[:, :TILE], by_row) + middle[:, :TILE] + last[:, :TILE]
         middle = 0.5 * middle[:, TILE:] + last[:, TILE : 2 * TILE]
         weighted = jnp.concatenate([start - first, middle - second, 0.5 * last[:, 2 * TILE :] - third], 1)
-        weighted = dot32(weighted, coefs, ((1,), (1,)))
+        weighted = dot_split(weighted, coefs, ((1,), (1,)))
         left_gram = held[:, size : size + block]
         right_gram = held[:, size + block :] + (weighted + weighted.T)
 

time: 112 us -> 112 us (level)
  transfers between devices with their start and end apart: 45 -> 45, of which waited for: 25 -> 25; matrix products, arithmetic and copies ran while one was open for 0% -> 0% of each run, Pallas kernels for 17% -> 18%
where the time goes in v1:
time: 112 us
  starting transfers between devices  47.1 us (42%)
  Pallas kernels  33.6 us (30%)
  waiting for transfers between devices  29.2 us (26%)
    ppermute x45, starting transfers between devices, swap(): return lax.ppermute(values, axis, [(i, i ^ bit) for i in range(size)])  47.1 us
    pallas_call x20, Pallas kernels, call(): pl.pallas_call(kernel, in_specs=specs or [VMEM] * len(inputs), out_specs=...  33.6 us
    ppermute x45, waiting for transfers between devices, swap(): return lax.ppermute(values, axis, [(i, i ^ bit) for i in range(size)])  29.2 us
  transfers between devices with their start and end apart: 45, of which 25 were waited for; matrix products, arithmetic and copies ran while one was open for 0% of the time, Pallas kernels for 18%

profile of v1, /device:TPU:0, one launch (start us, length us, event | category | flops | bytes accessed | tf_op | source)
XLA Modules:
  0.0 111.8 jit_solution(4279354399380702996)
XLA Ops:
  0.6 0.9 convert_element_type.3.rest_0_
  1.6 4.0 %collective-permute-start.3 = (bf16[64,768]{1,0:T(8,128)(2,1)S(1)}, bf16[64,768]{1,0:T(8,128)(2,1)S(1)}, u32[]{:S(2)}, u32[]{:S(2)}) collective-permute-start(bf16[64,768]{1,0:T(8,128)(2,1)S(1)} %convert_element_type.3.rest_0_), channel_id=1, source_target_pairs={{0,6},{1,7},{2,4},{3,5},{4,2},{5,3},{6,0},{7,1},{8,14},{9,15},{10,... | collective-permute-start | bytes 294920 | tf_op jit(solution)/shard_map/ppermute | solution.py:61
  5.6 0.5 collective-permute-start.2
  6.2 3.8 %shard_map.67.rest_8_.a_ref = bf16[768,6144]{1,0:T(8,128)(2,1)S(1)} custom-call(bf16[3072,6144]{1,0:T(8,128)(2,1)} %rest_2_.1), custom_call_target="tpu_custom_call" | custom-call | tf_op jit(solution)/shard_map/pallas_call | solution.py:50
  10.8 0.5 collective-permute-start.5
  11.3 0.8 collective-permute-done.4.rest_3_
  12.6 7.1 %shard_map.68 = (bf16[64,768]{1,0:T(8,128)(2,1)S(1)}, bf16[64,768]{1,0:T(8,128)(2,1)S(1)}, bf16[768,6144]{1,0:T(8,128)(2,1)S(1)}, bf16[768,6144]{1,0:T(8,128)(2,1)S(1)}, bf16[64,6144]{1,0:T(8,128)(2,1)S(1)}) custom-call(bf16[64,768]{1,0:T(8,128)(2,1)S(1)} %convert_element_type.3.rest_0_, bf16[64,768]{1,0:T(8,128)(2,1)S(1)} %collective-permute-done.rest_1_, ...), custom_call_target="tpu_custom_call" | custom-call | tf_op jit(solution)/shard_map/pallas_call | solution.py:50
  19.7 2.7 %collective-permute-start.8 = (bf16[64,768]{1,0:T(8,128)(2,1)S(1)}, bf16[64,768]{1,0:T(8,128)(2,1)S(1)}, u32[]{:S(2)}, u32[]{:S(2)}) collective-permute-start(bf16[64,768]{1,0:T(8,128)(2,1)S(1)} %get-tuple-element.58), channel_id=1, source_target_pairs={{0,16},{8,24},{16,0},{24,8},{1,17},{9,25},{17,1},{25,9},{2,18},{10... | collective-permute-start | bytes 294920 | tf_op jit(solution)/shard_map/ppermute | solution.py:61
  22.4 1.3 %collective-permute-start.9 = (bf16[64,768]{1,0:T(8,128)(2,1)S(1)}, bf16[64,768]{1,0:T(8,128)(2,1)S(1)}, u32[]{:S(2)}, u32[]{:S(2)}) collective-permute-start(bf16[64,768]{1,0:T(8,128)(2,1)S(1)} %get-tuple-element.59), channel_id=1, source_target_pairs={{0,24},{8,16},{16,8},{24,0},{1,25},{9,17},{17,9},{25,1},{2,26},{10... | collective-permute-start | bytes 294920 | tf_op jit(solution)/shard_map/ppermute | solution.py:61
  23.7 3.8 %shard_map.69 = (bf16[64,768]{1,0:T(8,128)(2,1)S(1)}, bf16[768,6144]{1,0:T(8,128)(2,1)S(1)}) custom-call(bf16[64,6144]{1,0:T(8,128)(2,1)S(1)} %get-tuple-element.53.rest_0_, bf16[768,6144]{1,0:T(8,128)(2,1)S(1)} %get-tuple-element.54.rest_1_.a_ref, bf16[3072,6144]{1,0:T(8,128)(2,1)} %rest_2_.1), custom_call_target="tpu_custom_call" | custom-call | tf_op jit(solution)/shard_map/pallas_call | solution.py:50
  27.8 3.4 %shard_map.70.rest_0_ = f32[64,768]{1,0:T(8,128)S(1)} custom-call(bf16[64,6144]{1,0:T(8,128)(2,1)S(1)} %get-tuple-element.53.rest_0_, bf16[768,6144]{1,0:T(8,128)(2,1)S(1)} %get-tuple-element.55.rest_1_.a_ref), custom_call_target="tpu_custom_call" | custom-call | tf_op jit(solution)/shard_map/pallas_call | solution.py:50
  31.7 0.6 collective-permute-done.7.rest_1_
  32.8 1.2 %collective-permute-done.10 = f32[32,384]{1,0:T(8,128)S(1)} collective-permute-done((f32[32,384]{1,0:T(8,128)S(1)}, f32[32,384]{1,0:T(8,128)S(1)}, u32[]{:S(2)}, u32[]{:S(2)}) %collective-permute-start.10) | collective-permute-done | bytes 49184 | tf_op jit(solution)/shard_map/ppermute | solution.py:61
  34.1 2.4 %collective-permute-start.13 = (f32[32,384]{1,0:T(8,128)S(1)}, f32[32,384]{1,0:T(8,128)S(1)}, u32[]{:S(2)}, u32[]{:S(2)}) collective-permute-start(f32[32,384]{1,0:T(8,128)S(1)} %add.51), channel_id=1, source_target_pairs={{0,6},{1,7},{2,4},{3,5},{4,2},{5,3},{6,0},{7,1},{8,14},{9,15},{10,... | collective-permute-start | bytes 147464 | tf_op jit(solution)/shard_map/ppermute | solution.py:61
  36.5 0.6 collective-permute-start.12
  37.1 0.6 collective-permute-start.11
  37.6 1.5 %collective-permute-done.13 = f32[32,384]{1,0:T(8,128)S(1)} collective-permute-done((f32[32,384]{1,0:T(8,128)S(1)}, f32[32,384]{1,0:T(8,128)S(1)}, u32[]{:S(2)}, u32[]{:S(2)}) %collective-permute-start.13) | collective-permute-done | bytes 49184 | tf_op jit(solution)/shard_map/ppermute | solution.py:61
  39.1 1.5 %collective-permute-done.12 = f32[32,384]{1,0:T(8,128)S(1)} collective-permute-done((f32[32,384]{1,0:T(8,128)S(1)}, f32[32,384]{1,0:T(8,128)S(1)}, u32[]{:S(2)}, u32[]{:S(2)}) %collective-permute-start.12) | collective-permute-done | bytes 49184 | tf_op jit(solution)/shard_map/ppermute | solution.py:61
  40.6 0.6 collective-permute-done.11
  41.2 3.2 %collective-permute-start.16 = (f32[32,384]{1,0:T(8,128)S(1)}, f32[32,384]{1,0:T(8,128)S(1)}, u32[]{:S(2)}, u32[]{:S(2)}) collective-permute-start(f32[32,384]{1,0:T(8,128)S(1)} %add_add_fusion.4), channel_id=1, source_target_pairs={{0,24},{8,16},{16,8},{24,0},{1,25},{9,17},{17,9},{25,1},{2,26},{10... | collective-permute-start | bytes 147464 | tf_op jit(solution)/shard_map/ppermute | solution.py:61
  44.3 1.3 %collective-permute-start.14 = (f32[32,384]{1,0:T(8,128)S(1)}, f32[32,384]{1,0:T(8,128)S(1)}, u32[]{:S(2)}, u32[]{:S(2)}) collective-permute-start(f32[32,384]{1,0:T(8,128)S(1)} %add_add_fusion.4), channel_id=1, source_target_pairs={{0,8},{8,0},{16,24},{24,16},{1,9},{9,1},{17,25},{25,17},{2,10},{10... | collective-permute-start | bytes 147464 | tf_op jit(solution)/shard_map/ppermute | solution.py:61
  45.6 1.5 %collective-permute-done.16 = f32[32,384]{1,0:T(8,128)S(1)} collective-permute-done((f32[32,384]{1,0:T(8,128)S(1)}, f32[32,384]{1,0:T(8,128)S(1)}, u32[]{:S(2)}, u32[]{:S(2)}) %collective-permute-start.16) | collective-permute-done | bytes 49184 | tf_op jit(solution)/shard_map/ppermute | solution.py:61
  47.2 2.2 %collective-permute-done.15 = f32[32,384]{1,0:T(8,128)S(1)} collective-permute-done((f32[32,384]{1,0:T(8,128)S(1)}, f32[32,384]{1,0:T(8,128)S(1)}, u32[]{:S(2)}, u32[]{:S(2)}) %collective-permute-start.15) | collective-permute-done | bytes 49184 | tf_op jit(solution)/shard_map/ppermute | solution.py:61
  49.4 1.2 %collective-permute-done.17.other_ref = f32[32,384]{1,0:T(8,128)S(1)} collective-permute-done((f32[32,384]{1,0:T(8,128)S(1)}, f32[32,384]{1,0:T(8,128)S(1)}, u32[]{:S(2)}, u32[]{:S(2)}) %collective-permute-start.17) | collective-permute-done | bytes 49184 | tf_op jit(solution)/shard_map/ppermute | solution.py:61
  50.6 0.7 shard_map.73
  51.4 0.5 collective-permute-start.20
  51.8 2.0 %collective-permute-start.19 = (bf16[64,768]{1,0:T(8,128)(2,1)S(1)}, bf16[64,768]{1,0:T(8,128)(2,1)S(1)}, u32[]{:S(2)}, u32[]{:S(2)}) collective-permute-start(bf16[64,768]{1,0:T(8,128)(2,1)S(1)} %get-tuple-element.68.p_ref), channel_id=1, source_target_pairs={{0,16},{8,24},{16,0},{24,8},{1,17},{9,25},{17,1},{25,9},{2,18},{10... | collective-permute-start | bytes 294920 | tf_op jit(solution)/shard_map/ppermute | solution.py:61
  53.8 2.0 %collective-permute-start.18 = (bf16[64,768]{1,0:T(8,128)(2,1)S(1)}, bf16[64,768]{1,0:T(8,128)(2,1)S(1)}, u32[]{:S(2)}, u32[]{:S(2)}) collective-permute-start(bf16[64,768]{1,0:T(8,128)(2,1)S(1)} %get-tuple-element.68.p_ref), channel_id=1, source_target_pairs={{0,24},{8,16},{16,8},{24,0},{1,25},{9,17},{17,9},{25,1},{2,26},{10... | collective-permute-start | bytes 294920 | tf_op jit(solution)/shard_map/ppermute | solution.py:61
  55.8 1.7 %shard_map.74.rest_0_ = f32[64,6144]{1,0:T(8,128)S(1)} custom-call(bf16[64,768]{1,0:T(8,128)(2,1)S(1)} %get-tuple-element.68.p_ref, bf16[768,6144]{1,0:T(8,128)(2,1)S(1)} %get-tuple-element.55.rest_1_.a_ref), custom_call_target="tpu_custom_call" | custom-call | tf_op jit(solution)/shard_map/pallas_call | solution.py:50
  57.6 0.8 collective-permute-done.20.p_ref
  58.4 1.7 %shard_map.75.rest_0_ = f32[64,6144]{1,0:T(8,128)S(1)} custom-call(bf16[64,768]{1,0:T(8,128)(2,1)S(1)} %collective-permute-done.20.p_ref, bf16[768,6144]{1,0:T(8,128)(2,1)S(1)} %get-tuple-element.54.rest_1_.a_ref, f32[64,6144]{1,0:T(8,128)S(1)} %shard_map.74.rest_0_), custom_call_target="tpu_custom_call" | custom-call | tf_op jit(solution)/shard_map/pallas_call | solution.py:50
  60.2 1.7 %shard_map.76.rest_2_ = f32[64,6144]{1,0:T(8,128)S(1)} custom-call(bf16[64,768]{1,0:T(8,128)(2,1)S(1)} %collective-permute-done.19.p_ref, bf16[768,6144]{1,0:T(8,128)(2,1)S(1)} %shard_map.67.rest_8_.a_ref, f32[64,6144]{1,0:T(8,128)S(1)} %shard_map.75.rest_0_), custom_call_target="tpu_custom_call" | custom-call | tf_op jit(solution)/shard_map/pallas_call | solution.py:50
  62.1 0.8 shard_map.78
  63.0 0.8 shard_map.77.mine_ref
  63.8 1.2 %collective-permute-done.21.theirs_ref = f32[3,64,768]{2,1,0:T(8,128)S(1)} collective-permute-done((f32[3,64,768]{2,1,0:T(8,128)S(1)}, f32[3,64,768]{2,1,0:T(8,128)S(1)}, u32[]{:S(2)}, u32[]{:S(2)}) %collective-permute-start.21) | collective-permute-done | bytes 589856 | tf_op jit(solution)/shard_map/ppermute | solution.py:61
  65.0 0.6 shard_map.80
  65.8 1.5 %shard_map.81 = (bf16[384,768]{1,0:T(8,128)(2,1)S(1)}, bf16[384,768]{1,0:T(8,128)(2,1)S(1)}, bf16[768,768]{1,0:T(8,128)(2,1)S(1)}, f32[128,384]{1,0:T(8,128)S(1)}, f32[128,384]{1,0:T(8,128)S(1)}) custom-call(f32[320,768]{1,0:T(8,128)S(1)} %copy-done.1, f32[64,768]{1,0:T(8,128)S(1)} %copy-done.2), custom_call_target="tpu_custom_call" | custom-call | tf_op jit(solution)/shard_map/pallas_call | solution.py:50
  67.7 0.5 collective-permute-start.23
  68.3 1.5 %collective-permute-start.24 = (bf16[64,768]{1,0:T(8,128)(2,1)S(1)}, bf16[64,768]{1,0:T(8,128)(2,1)S(1)}, u32[]{:S(2)}, u32[]{:S(2)}) collective-permute-start(bf16[64,768]{1,0:T(8,128)(2,1)S(1)} %get-tuple-element.77), channel_id=1, source_target_pairs={{0,4},{1,5},{2,6},{3,7},{4,0},{5,1},{6,2},{7,3},{8,12},{9,13},{10,... | collective-permute-start | bytes 294920 | tf_op jit(solution)/shard_map/ppermute | solution.py:61
  69.8 1.4 %collective-permute-start.25 = (bf16[64,768]{1,0:T(8,128)(2,1)S(1)}, bf16[64,768]{1,0:T(8,128)(2,1)S(1)}, u32[]{:S(2)}, u32[]{:S(2)}) collective-permute-start(bf16[64,768]{1,0:T(8,128)(2,1)S(1)} %get-tuple-element.78), channel_id=1, source_target_pairs={{0,6},{1,7},{2,4},{3,5},{4,2},{5,3},{6,0},{7,1},{8,14},{9,15},{10,... | collective-permute-start | bytes 294920 | tf_op jit(solution)/shard_map/ppermute | solution.py:61
  71.2 2.0 %collective-permute-done.23.rest_2_ = bf16[64,768]{1,0:T(8,128)(2,1)S(1)} collective-permute-done((bf16[64,768]{1,0:T(8,128)(2,1)S(1)}, bf16[64,768]{1,0:T(8,128)(2,1)S(1)}, u32[]{:S(2)}, u32[]{:S(2)}) %collective-permute-start.23) | collective-permute-done | bytes 98336 | tf_op jit(solution)/shard_map/ppermute | solution.py:61
  73.2 0.8 collective-permute-done.24.rest_3_
  74.1 1.6 %collective-permute-done.25.rest_4_ = bf16[64,768]{1,0:T(8,128)(2,1)S(1)} collective-permute-done((bf16[64,768]{1,0:T(8,128)(2,1)S(1)}, bf16[64,768]{1,0:T(8,128)(2,1)S(1)}, u32[]{:S(2)}, u32[]{:S(2)}) %collective-permute-start.25) | collective-permute-done | bytes 98336 | tf_op jit(solution)/shard_map/ppermute | solution.py:61
  75.6 0.6 shard_map.82
  76.3 1.2 %collective-permute-start.35 = (f32[32,384]{1,0:T(8,128)S(1)}, f32[32,384]{1,0:T(8,128)S(1)}, u32[]{:S(2)}, u32[]{:S(2)}) collective-permute-start(f32[32,384]{1,0:T(8,128)S(1)} %get-tuple-element.91), channel_id=1, source_target_pairs={{0,2},{1,3},{2,0},{3,1},{4,6},{5,7},{6,4},{7,5},{8,10},{9,11},{10,... | collective-permute-start | bytes 147464 | tf_op jit(solution)/shard_map/ppermute | solution.py:61
  77.6 1.8 %collective-permute-start.29 = (f32[32,512]{1,0:T(8,128)S(1)}, f32[32,512]{1,0:T(8,128)S(1)}, u32[]{:S(2)}, u32[]{:S(2)}) collective-permute-start(f32[32,512]{1,0:T(8,128)S(1)} %add.58), channel_id=1, source_target_pairs={{0,6},{1,7},{2,4},{3,5},{4,2},{5,3},{6,0},{7,1},{8,14},{9,15},{10,... | collective-permute-start | bytes 196616 | tf_op jit(solution)/shard_map/ppermute | solution.py:61
  79.4 0.8 collective-permute-start.28
  80.2 0.9 collective-permute-start.27
  81.1 1.2 %collective-permute-start.36 = (f32[32,384]{1,0:T(8,128)S(1)}, f32[32,384]{1,0:T(8,128)S(1)}, u32[]{:S(2)}, u32[]{:S(2)}) collective-permute-start(f32[32,384]{1,0:T(8,128)S(1)} %get-tuple-element.92), channel_id=1, source_target_pairs={{0,4},{1,5},{2,6},{3,7},{4,0},{5,1},{6,2},{7,3},{8,12},{9,13},{10,... | collective-permute-start | bytes 147464 | tf_op jit(solution)/shard_map/ppermute | solution.py:61
  82.4 1.4 %collective-permute-start.37 = (f32[32,384]{1,0:T(8,128)S(1)}, f32[32,384]{1,0:T(8,128)S(1)}, u32[]{:S(2)}, u32[]{:S(2)}) collective-permute-start(f32[32,384]{1,0:T(8,128)S(1)} %get-tuple-element.93), channel_id=1, source_target_pairs={{0,6},{1,7},{2,4},{3,5},{4,2},{5,3},{6,0},{7,1},{8,14},{9,15},{10,... | collective-permute-start | bytes 147464 | tf_op jit(solution)/shard_map/ppermute | solution.py:61
  83.7 1.7 %collective-permute-done.36.c = f32[32,384]{1,0:T(8,128)S(1)} collective-permute-done((f32[32,384]{1,0:T(8,128)S(1)}, f32[32,384]{1,0:T(8,128)S(1)}, u32[]{:S(2)}, u32[]{:S(2)}) %collective-permute-start.36) | collective-permute-done | bytes 49184 | tf_op jit(solution)/shard_map/ppermute | solution.py:61
  85.4 1.9 %collective-permute-done.37.d = f32[32,384]{1,0:T(8,128)S(1)} collective-permute-done((f32[32,384]{1,0:T(8,128)S(1)}, f32[32,384]{1,0:T(8,128)S(1)}, u32[]{:S(2)}, u32[]{:S(2)}) %collective-permute-start.37) | collective-permute-done | bytes 49184 | tf_op jit(solution)/shard_map/ppermute | solution.py:61
  87.4 4.6 %collective-permute-start.40 = (f32[32,384]{1,0:T(8,128)S(1)}, f32[32,384]{1,0:T(8,128)S(1)}, u32[]{:S(2)}, u32[]{:S(2)}) collective-permute-start(f32[32,384]{1,0:T(8,128)S(1)} %shard_map.84), channel_id=1, source_target_pairs={{0,24},{8,16},{16,8},{24,0},{1,25},{9,17},{17,9},{25,1},{2,26},{10... | collective-permute-start | bytes 147464 | tf_op jit(solution)/shard_map/ppermute | solution.py:61
  92.0 0.6 collective-permute-start.38
  92.7 3.8 %collective-permute-start.32 = (f32[32,512]{1,0:T(8,128)S(1)}, f32[32,512]{1,0:T(8,128)S(1)}, u32[]{:S(2)}, u32[]{:S(2)}) collective-permute-start(f32[32,512]{1,0:T(8,128)S(1)} %add_add_fusion.1), channel_id=1, source_target_pairs={{0,24},{8,16},{16,8},{24,0},{1,25},{9,17},{17,9},{25,1},{2,26},{10... | collective-permute-start | bytes 196616 | tf_op jit(solution)/shard_map/ppermute | solution.py:61
  96.5 0.6 collective-permute-start.30
  97.1 1.1 collective-permute-done.39
  98.3 1.2 %collective-permute-done.41.other_ref = f32[32,384]{1,0:T(8,128)S(1)} collective-permute-done((f32[32,384]{1,0:T(8,128)S(1)}, f32[32,384]{1,0:T(8,128)S(1)}, u32[]{:S(2)}, u32[]{:S(2)}) %collective-permute-start.41) | collective-permute-done | bytes 49184 | tf_op jit(solution)/shard_map/ppermute | solution.py:61
  99.5 1.2 %collective-permute-start.44 = (f32[64,384]{1,0:T(8,128)S(1)}, f32[64,384]{1,0:T(8,128)S(1)}, u32[]{:S(2)}, u32[]{:S(2)}) collective-permute-start(f32[64,384]{1,0:T(8,128)S(1)} %shard_map.85.q0), channel_id=1, source_target_pairs={{0,6},{1,7},{2,4},{3,5},{4,2},{5,3},{6,0},{7,1},{8,14},{9,15},{10,... | collective-permute-start | bytes 294920 | tf_op jit(solution)/shard_map/ppermute | solution.py:61
  100.8 1.2 %collective-permute-start.43 = (f32[64,384]{1,0:T(8,128)S(1)}, f32[64,384]{1,0:T(8,128)S(1)}, u32[]{:S(2)}, u32[]{:S(2)}) collective-permute-start(f32[64,384]{1,0:T(8,128)S(1)} %shard_map.85.q0), channel_id=1, source_target_pairs={{0,4},{1,5},{2,6},{3,7},{4,0},{5,1},{6,2},{7,3},{8,12},{9,13},{10,... | collective-permute-start | bytes 294920 | tf_op jit(solution)/shard_map/ppermute | solution.py:61
  102.0 1.1 collective-permute-start.42
  103.2 3.0 %collective-permute-done.44.q3 = f32[64,384]{1,0:T(8,128)S(1)} collective-permute-done((f32[64,384]{1,0:T(8,128)S(1)}, f32[64,384]{1,0:T(8,128)S(1)}, u32[]{:S(2)}, u32[]{:S(2)}) %collective-permute-start.44) | collective-permute-done | bytes 98336 | tf_op jit(solution)/shard_map/ppermute | solution.py:61
  106.2 1.3 %collective-permute-done.43.q2 = f32[64,384]{1,0:T(8,128)S(1)} collective-permute-done((f32[64,384]{1,0:T(8,128)S(1)}, f32[64,384]{1,0:T(8,128)S(1)}, u32[]{:S(2)}, u32[]{:S(2)}) %collective-permute-start.43) | collective-permute-done | bytes 98336 | tf_op jit(solution)/shard_map/ppermute | solution.py:61
  107.5 4.3 %shard_map.86 = (f32[64,768]{1,0:T(8,128)}, f32[64,768]{1,0:T(8,128)}, f32[2,64,64]{2,1,0:T(8,128)}) custom-call(f32[64,768]{1,0:T(8,128)S(1)} %get-tuple-element.83.image_ref, bf16[384,768]{1,0:T(8,128)(2,1)S(1)} %get-tuple-element.84.high_ref, bf16[384,768]{1,0:T(8,128)(2,1)S(1)} %get-tuple-element.85.low_ref, f32[32,512]{1,0:T(8,128)S(1)} %add_add_fusion.mine_ref, ...), custom_call_target="tpu_custom_call" | custom-call | tf_op jit(solution)/shard_map/pallas_call | solution.py:50
  (60 shorter events, 4.1 us)
Async XLA Ops:
  1.6 8.4 %collective-permute-start.3 = (bf16[64,768]{1,0:T(8,128)(2,1)S(1)}, bf16[64,768]{1,0:T(8,128)(2,1)S(1)}, u32[]{:S(2)}, u32[]{:S(2)}) collective-permute-start(bf16[64,768]{1,0:T(8,128)(2,1)S(1)} %convert_element_type.3.rest_0_), channel_id=1, source_target_pairs={{0,6},{1,7},{2,4},{3,5},{4,2},{5,3},{6,0},{7,1},{8,14},{9,15},{10,... | collective-permute-start | bytes 294920 | tf_op jit(solution)/shard_map/ppermute | solution.py:61
  5.6 4.9 %collective-permute-start.2 = (bf16[64,768]{1,0:T(8,128)(2,1)S(1)}, bf16[64,768]{1,0:T(8,128)(2,1)S(1)}, u32[]{:S(2)}, u32[]{:S(2)}) collective-permute-start(bf16[64,768]{1,0:T(8,128)(2,1)S(1)} %convert_element_type.3.rest_0_), channel_id=1, source_target_pairs={{0,4},{1,5},{2,6},{3,7},{4,0},{5,1},{6,2},{7,3},{8,12},{9,13},{10,... | collective-permute-start | bytes 294920 | tf_op jit(solution)/shard_map/ppermute | solution.py:61
  6.1 4.7 %collective-permute-start.1 = (bf16[64,768]{1,0:T(8,128)(2,1)S(1)}, bf16[64,768]{1,0:T(8,128)(2,1)S(1)}, u32[]{:S(2)}, u32[]{:S(2)}) collective-permute-start(bf16[64,768]{1,0:T(8,128)(2,1)S(1)} %convert_element_type.3.rest_0_), channel_id=1, source_target_pairs={{0,2},{1,3},{2,0},{3,1},{4,6},{5,7},{6,4},{7,5},{8,10},{9,11},{10,... | collective-permute-start | bytes 294920 | tf_op jit(solution)/shard_map/ppermute | solution.py:61
  6.2 5.1 %collective-permute-start = (bf16[64,768]{1,0:T(8,128)(2,1)S(1)}, bf16[64,768]{1,0:T(8,128)(2,1)S(1)}, u32[]{:S(2)}, u32[]{:S(2)}) collective-permute-start(bf16[64,768]{1,0:T(8,128)(2,1)S(1)} %convert_element_type.3.rest_0_), channel_id=1, source_target_pairs={{0,1},{1,0},{2,3},{3,2},{4,5},{5,4},{6,7},{7,6},{8,9},{9,8},{10,11... | collective-permute-start | bytes 294920 | tf_op jit(solution)/shard_map/ppermute | solution.py:61
  10.8 1.3 %collective-permute-start.4 = (bf16[64,768]{1,0:T(8,128)(2,1)S(1)}, bf16[64,768]{1,0:T(8,128)(2,1)S(1)}, u32[]{:S(2)}, u32[]{:S(2)}) collective-permute-start(bf16[64,768]{1,0:T(8,128)(2,1)S(1)} %collective-permute-done.1.rest_2_), channel_id=1, source_target_pairs={{0,1},{1,0},{2,3},{3,2},{4,5},{5,4},{6,7},{7,6},{8,9},{9,8},{10,11... | collective-permute-start | bytes 294920 | tf_op jit(solution)/shard_map/ppermute | solution.py:61
  10.8 1.5 %collective-permute-start.5 = (bf16[64,768]{1,0:T(8,128)(2,1)S(1)}, bf16[64,768]{1,0:T(8,128)(2,1)S(1)}, u32[]{:S(2)}, u32[]{:S(2)}) collective-permute-start(bf16[64,768]{1,0:T(8,128)(2,1)S(1)} %collective-permute-done.2.rest_4_), channel_id=1, source_target_pairs={{0,1},{1,0},{2,3},{3,2},{4,5},{5,4},{6,7},{7,6},{8,9},{9,8},{10,11... | collective-permute-start | bytes 294920 | tf_op jit(solution)/shard_map/ppermute | solution.py:61
  11.3 1.3 %collective-permute-start.6 = (bf16[64,768]{1,0:T(8,128)(2,1)S(1)}, bf16[64,768]{1,0:T(8,128)(2,1)S(1)}, u32[]{:S(2)}, u32[]{:S(2)}) collective-permute-start(bf16[64,768]{1,0:T(8,128)(2,1)S(1)} %collective-permute-done.3.rest_6_), channel_id=1, source_target_pairs={{0,1},{1,0},{2,3},{3,2},{4,5},{5,4},{6,7},{7,6},{8,9},{9,8},{10,11... | collective-permute-start | bytes 294920 | tf_op jit(solution)/shard_map/ppermute | solution.py:61
  19.7 12.0 %collective-permute-start.8 = (bf16[64,768]{1,0:T(8,128)(2,1)S(1)}, bf16[64,768]{1,0:T(8,128)(2,1)S(1)}, u32[]{:S(2)}, u32[]{:S(2)}) collective-permute-start(bf16[64,768]{1,0:T(8,128)(2,1)S(1)} %get-tuple-element.58), channel_id=1, source_target_pairs={{0,16},{8,24},{16,0},{24,8},{1,17},{9,25},{17,1},{25,9},{2,18},{10... | collective-permute-start | bytes 294920 | tf_op jit(solution)/shard_map/ppermute | solution.py:61
  22.4 9.3 %collective-permute-start.9 = (bf16[64,768]{1,0:T(8,128)(2,1)S(1)}, bf16[64,768]{1,0:T(8,128)(2,1)S(1)}, u32[]{:S(2)}, u32[]{:S(2)}) collective-permute-start(bf16[64,768]{1,0:T(8,128)(2,1)S(1)} %get-tuple-element.59), channel_id=1, source_target_pairs={{0,24},{8,16},{16,8},{24,0},{1,25},{9,17},{17,9},{25,1},{2,26},{10... | collective-permute-start | bytes 294920 | tf_op jit(solution)/shard_map/ppermute | solution.py:61
  27.5 3.7 %copy-start = (f32[320,768]{1,0:T(8,128)S(1)}, f32[320,768]{1,0:T(8,128)}, u32[]{:S(2)}) copy-start(f32[320,768]{1,0:T(8,128)} %rest_0_) | copy-start | bytes 2949124
  27.5 4.8 %collective-permute-start.7 = (bf16[64,768]{1,0:T(8,128)(2,1)S(1)}, bf16[64,768]{1,0:T(8,128)(2,1)S(1)}, u32[]{:S(2)}, u32[]{:S(2)}) collective-permute-start(bf16[64,768]{1,0:T(8,128)(2,1)S(1)} %get-tuple-element.57), channel_id=1, source_target_pairs={{0,8},{8,0},{16,24},{24,16},{1,9},{9,1},{17,25},{25,17},{2,10},{10... | collective-permute-start | bytes 294920 | tf_op jit(solution)/shard_map/ppermute | solution.py:61
  32.7 1.3 %collective-permute-start.10 = (f32[32,384]{1,0:T(8,128)S(1)}, f32[32,384]{1,0:T(8,128)S(1)}, u32[]{:S(2)}, u32[]{:S(2)}) collective-permute-start(f32[32,384]{1,0:T(8,128)S(1)} %get-tuple-element.67), channel_id=1, source_target_pairs={{0,1},{1,0},{2,3},{3,2},{4,5},{5,4},{6,7},{7,6},{8,9},{9,8},{10,11... | collective-permute-start | bytes 147464 | tf_op jit(solution)/shard_map/ppermute | solution.py:61
  34.1 5.1 %collective-permute-start.13 = (f32[32,384]{1,0:T(8,128)S(1)}, f32[32,384]{1,0:T(8,128)S(1)}, u32[]{:S(2)}, u32[]{:S(2)}) collective-permute-start(f32[32,384]{1,0:T(8,128)S(1)} %add.51), channel_id=1, source_target_pairs={{0,6},{1,7},{2,4},{3,5},{4,2},{5,3},{6,0},{7,1},{8,14},{9,15},{10,... | collective-permute-start | bytes 147464 | tf_op jit(solution)/shard_map/ppermute | solution.py:61
  36.5 4.1 %collective-permute-start.12 = (f32[32,384]{1,0:T(8,128)S(1)}, f32[32,384]{1,0:T(8,128)S(1)}, u32[]{:S(2)}, u32[]{:S(2)}) collective-permute-start(f32[32,384]{1,0:T(8,128)S(1)} %add.51), channel_id=1, source_target_pairs={{0,4},{1,5},{2,6},{3,7},{4,0},{5,1},{6,2},{7,3},{8,12},{9,13},{10,... | collective-permute-start | bytes 147464 | tf_op jit(solution)/shard_map/ppermute | solution.py:61
  37.1 4.1 %collective-permute-start.11 = (f32[32,384]{1,0:T(8,128)S(1)}, f32[32,384]{1,0:T(8,128)S(1)}, u32[]{:S(2)}, u32[]{:S(2)}) collective-permute-start(f32[32,384]{1,0:T(8,128)S(1)} %add.51), channel_id=1, source_target_pairs={{0,2},{1,3},{2,0},{3,1},{4,6},{5,7},{6,4},{7,5},{8,10},{9,11},{10,... | collective-permute-start | bytes 147464 | tf_op jit(solution)/shard_map/ppermute | solution.py:61
  41.2 6.0 %collective-permute-start.16 = (f32[32,384]{1,0:T(8,128)S(1)}, f32[32,384]{1,0:T(8,128)S(1)}, u32[]{:S(2)}, u32[]{:S(2)}) collective-permute-start(f32[32,384]{1,0:T(8,128)S(1)} %add_add_fusion.4), channel_id=1, source_target_pairs={{0,24},{8,16},{16,8},{24,0},{1,25},{9,17},{17,9},{25,1},{2,26},{10... | collective-permute-start | bytes 147464 | tf_op jit(solution)/shard_map/ppermute | solution.py:61
  44.3 5.0 %collective-permute-start.15 = (f32[32,384]{1,0:T(8,128)S(1)}, f32[32,384]{1,0:T(8,128)S(1)}, u32[]{:S(2)}, u32[]{:S(2)}) collective-permute-start(f32[32,384]{1,0:T(8,128)S(1)} %add_add_fusion.4), channel_id=1, source_target_pairs={{0,16},{8,24},{16,0},{24,8},{1,17},{9,25},{17,1},{25,9},{2,18},{10... | collective-permute-start | bytes 147464 | tf_op jit(solution)/shard_map/ppermute | solution.py:61
  44.3 5.0 %collective-permute-start.14 = (f32[32,384]{1,0:T(8,128)S(1)}, f32[32,384]{1,0:T(8,128)S(1)}, u32[]{:S(2)}, u32[]{:S(2)}) collective-permute-start(f32[32,384]{1,0:T(8,128)S(1)} %add_add_fusion.4), channel_id=1, source_target_pairs={{0,8},{8,0},{16,24},{24,16},{1,9},{9,1},{17,25},{25,17},{2,10},{10... | collective-permute-start | bytes 147464 | tf_op jit(solution)/shard_map/ppermute | solution.py:61
  49.3 1.3 %collective-permute-start.17 = (f32[32,384]{1,0:T(8,128)S(1)}, f32[32,384]{1,0:T(8,128)S(1)}, u32[]{:S(2)}, u32[]{:S(2)}) collective-permute-start(f32[32,384]{1,0:T(8,128)S(1)} %add_add_fusion.3.mine_ref), channel_id=1, source_target_pairs={{0,1},{1,0},{2,3},{3,2},{4,5},{5,4},{6,7},{7,6},{8,9},{9,8},{10,11... | collective-permute-start | bytes 147464 | tf_op jit(solution)/shard_map/ppermute | solution.py:61
  51.4 7.0 %collective-permute-start.20 = (bf16[64,768]{1,0:T(8,128)(2,1)S(1)}, bf16[64,768]{1,0:T(8,128)(2,1)S(1)}, u32[]{:S(2)}, u32[]{:S(2)}) collective-permute-start(bf16[64,768]{1,0:T(8,128)(2,1)S(1)} %get-tuple-element.68.p_ref), channel_id=1, source_target_pairs={{0,8},{8,0},{16,24},{24,16},{1,9},{9,1},{17,25},{25,17},{2,10},{10... | collective-permute-start | bytes 294920 | tf_op jit(solution)/shard_map/ppermute | solution.py:61
  51.8 8.3 %collective-permute-start.19 = (bf16[64,768]{1,0:T(8,128)(2,1)S(1)}, bf16[64,768]{1,0:T(8,128)(2,1)S(1)}, u32[]{:S(2)}, u32[]{:S(2)}) collective-permute-start(bf16[64,768]{1,0:T(8,128)(2,1)S(1)} %get-tuple-element.68.p_ref), channel_id=1, source_target_pairs={{0,16},{8,24},{16,0},{24,8},{1,17},{9,25},{17,1},{25,9},{2,18},{10... | collective-permute-start | bytes 294920 | tf_op jit(solution)/shard_map/ppermute | solution.py:61
  53.8 8.3 %collective-permute-start.18 = (bf16[64,768]{1,0:T(8,128)(2,1)S(1)}, bf16[64,768]{1,0:T(8,128)(2,1)S(1)}, u32[]{:S(2)}, u32[]{:S(2)}) collective-permute-start(bf16[64,768]{1,0:T(8,128)(2,1)S(1)} %get-tuple-element.68.p_ref), channel_id=1, source_target_pairs={{0,24},{8,16},{16,8},{24,0},{1,25},{9,17},{17,9},{25,1},{2,26},{10... | collective-permute-start | bytes 294920 | tf_op jit(solution)/shard_map/ppermute | solution.py:61
  62.9 2.9 %copy-start.1 = (f32[320,768]{1,0:T(8,128)S(1)}, f32[320,768]{1,0:T(8,128)}, u32[]{:S(2)}) copy-start(f32[320,768]{1,0:T(8,128)} %rest_0_.1) | copy-start | bytes 2949124
  62.9 2.9 %copy-start.2 = (f32[64,768]{1,0:T(8,128)S(1)}, f32[64,768]{1,0:T(8,128)}, u32[]{:S(2)}) copy-start(f32[64,768]{1,0:T(8,128)} %rest_1_) | copy-start | bytes 589828
  62.9 2.1 %collective-permute-start.21 = (f32[3,64,768]{2,1,0:T(8,128)S(1)}, f32[3,64,768]{2,1,0:T(8,128)S(1)}, u32[]{:S(2)}, u32[]{:S(2)}) collective-permute-start(f32[3,64,768]{2,1,0:T(8,128)S(1)} %shard_map.78), channel_id=1, source_target_pairs={{0,1},{1,0},{2,3},{3,2},{4,5},{5,4},{6,7},{7,6},{8,9},{9,8},{10,11... | collective-permute-start | bytes 1769480 | tf_op jit(solution)/shard_map/ppermute | solution.py:61
  65.6 10.1 %collective-permute-start.22 = (f32[1,64,768]{2,1,0:T(8,128)S(1)}, f32[1,64,768]{2,1,0:T(8,128)S(1)}, u32[]{:S(2)}, u32[]{:S(2)}) collective-permute-start(f32[1,64,768]{2,1,0:T(8,128)S(1)} %get-tuple-element.75), channel_id=1, source_target_pairs={{0,1},{1,0},{2,3},{3,2},{4,5},{5,4},{6,7},{7,6},{8,9},{9,8},{10,11... | collective-permute-start | bytes 589832 | tf_op jit(solution)/shard_map/ppermute | solution.py:61
  67.3 9.0 %collective-permute-start.34 = (f32[128,384]{1,0:T(8,128)S(1)}, f32[128,384]{1,0:T(8,128)S(1)}, u32[]{:S(2)}, u32[]{:S(2)}) collective-permute-start(f32[128,384]{1,0:T(8,128)S(1)} %get-tuple-element.89), channel_id=1, source_target_pairs={{0,1},{1,0},{2,3},{3,2},{4,5},{5,4},{6,7},{7,6},{8,9},{9,8},{10,11... | collective-permute-start | bytes 589832 | tf_op jit(solution)/shard_map/ppermute | solution.py:61
  67.7 5.5 %collective-permute-start.23 = (bf16[64,768]{1,0:T(8,128)(2,1)S(1)}, bf16[64,768]{1,0:T(8,128)(2,1)S(1)}, u32[]{:S(2)}, u32[]{:S(2)}) collective-permute-start(bf16[64,768]{1,0:T(8,128)(2,1)S(1)} %get-tuple-element.76), channel_id=1, source_target_pairs={{0,2},{1,3},{2,0},{3,1},{4,6},{5,7},{6,4},{7,5},{8,10},{9,11},{10,... | collective-permute-start | bytes 294920 | tf_op jit(solution)/shard_map/ppermute | solution.py:61
  68.3 5.8 %collective-permute-start.24 = (bf16[64,768]{1,0:T(8,128)(2,1)S(1)}, bf16[64,768]{1,0:T(8,128)(2,1)S(1)}, u32[]{:S(2)}, u32[]{:S(2)}) collective-permute-start(bf16[64,768]{1,0:T(8,128)(2,1)S(1)} %get-tuple-element.77), channel_id=1, source_target_pairs={{0,4},{1,5},{2,6},{3,7},{4,0},{5,1},{6,2},{7,3},{8,12},{9,13},{10,... | collective-permute-start | bytes 294920 | tf_op jit(solution)/shard_map/ppermute | solution.py:61
  69.8 5.8 %collective-permute-start.25 = (bf16[64,768]{1,0:T(8,128)(2,1)S(1)}, bf16[64,768]{1,0:T(8,128)(2,1)S(1)}, u32[]{:S(2)}, u32[]{:S(2)}) collective-permute-start(bf16[64,768]{1,0:T(8,128)(2,1)S(1)} %get-tuple-element.78), channel_id=1, source_target_pairs={{0,6},{1,7},{2,4},{3,5},{4,2},{5,3},{6,0},{7,1},{8,14},{9,15},{10,... | collective-permute-start | bytes 294920 | tf_op jit(solution)/shard_map/ppermute | solution.py:61
  76.2 1.4 %collective-permute-start.26 = (f32[32,512]{1,0:T(8,128)S(1)}, f32[32,512]{1,0:T(8,128)S(1)}, u32[]{:S(2)}, u32[]{:S(2)}) collective-permute-start(f32[32,512]{1,0:T(8,128)S(1)} %get-tuple-element.87), channel_id=1, source_target_pairs={{0,1},{1,0},{2,3},{3,2},{4,5},{5,4},{6,7},{7,6},{8,9},{9,8},{10,11... | collective-permute-start | bytes 196616 | tf_op jit(solution)/shard_map/ppermute | solution.py:61
  76.3 6.0 %collective-permute-start.35 = (f32[32,384]{1,0:T(8,128)S(1)}, f32[32,384]{1,0:T(8,128)S(1)}, u32[]{:S(2)}, u32[]{:S(2)}) collective-permute-start(f32[32,384]{1,0:T(8,128)S(1)} %get-tuple-element.91), channel_id=1, source_target_pairs={{0,2},{1,3},{2,0},{3,1},{4,6},{5,7},{6,4},{7,5},{8,10},{9,11},{10,... | collective-permute-start | bytes 147464 | tf_op jit(solution)/shard_map/ppermute | solution.py:61
  77.6 14.4 %collective-permute-start.29 = (f32[32,512]{1,0:T(8,128)S(1)}, f32[32,512]{1,0:T(8,128)S(1)}, u32[]{:S(2)}, u32[]{:S(2)}) collective-permute-start(f32[32,512]{1,0:T(8,128)S(1)} %add.58), channel_id=1, source_target_pairs={{0,6},{1,7},{2,4},{3,5},{4,2},{5,3},{6,0},{7,1},{8,14},{9,15},{10,... | collective-permute-start | bytes 196616 | tf_op jit(solution)/shard_map/ppermute | solution.py:61
  79.4 13.2 %collective-permute-start.28 = (f32[32,512]{1,0:T(8,128)S(1)}, f32[32,512]{1,0:T(8,128)S(1)}, u32[]{:S(2)}, u32[]{:S(2)}) collective-permute-start(f32[32,512]{1,0:T(8,128)S(1)} %add.58), channel_id=1, source_target_pairs={{0,4},{1,5},{2,6},{3,7},{4,0},{5,1},{6,2},{7,3},{8,12},{9,13},{10,... | collective-permute-start | bytes 196616 | tf_op jit(solution)/shard_map/ppermute | solution.py:61
  80.2 12.4 %collective-permute-start.27 = (f32[32,512]{1,0:T(8,128)S(1)}, f32[32,512]{1,0:T(8,128)S(1)}, u32[]{:S(2)}, u32[]{:S(2)}) collective-permute-start(f32[32,512]{1,0:T(8,128)S(1)} %add.58), channel_id=1, source_target_pairs={{0,2},{1,3},{2,0},{3,1},{4,6},{5,7},{6,4},{7,5},{8,10},{9,11},{10,... | collective-permute-start | bytes 196616 | tf_op jit(solution)/shard_map/ppermute | solution.py:61
  81.1 4.3 %collective-permute-start.36 = (f32[32,384]{1,0:T(8,128)S(1)}, f32[32,384]{1,0:T(8,128)S(1)}, u32[]{:S(2)}, u32[]{:S(2)}) collective-permute-start(f32[32,384]{1,0:T(8,128)S(1)} %get-tuple-element.92), channel_id=1, source_target_pairs={{0,4},{1,5},{2,6},{3,7},{4,0},{5,1},{6,2},{7,3},{8,12},{9,13},{10,... | collective-permute-start | bytes 147464 | tf_op jit(solution)/shard_map/ppermute | solution.py:61
  82.4 5.0 %collective-permute-start.37 = (f32[32,384]{1,0:T(8,128)S(1)}, f32[32,384]{1,0:T(8,128)S(1)}, u32[]{:S(2)}, u32[]{:S(2)}) collective-permute-start(f32[32,384]{1,0:T(8,128)S(1)} %get-tuple-element.93), channel_id=1, source_target_pairs={{0,6},{1,7},{2,4},{3,5},{4,2},{5,3},{6,0},{7,1},{8,14},{9,15},{10,... | collective-permute-start | bytes 147464 | tf_op jit(solution)/shard_map/ppermute | solution.py:61
  87.4 9.1 %collective-permute-start.40 = (f32[32,384]{1,0:T(8,128)S(1)}, f32[32,384]{1,0:T(8,128)S(1)}, u32[]{:S(2)}, u32[]{:S(2)}) collective-permute-start(f32[32,384]{1,0:T(8,128)S(1)} %shard_map.84), channel_id=1, source_target_pairs={{0,24},{8,16},{16,8},{24,0},{1,25},{9,17},{17,9},{25,1},{2,26},{10... | collective-permute-start | bytes 147464 | tf_op jit(solution)/shard_map/ppermute | solution.py:61
  92.0 6.2 %collective-permute-start.39 = (f32[32,384]{1,0:T(8,128)S(1)}, f32[32,384]{1,0:T(8,128)S(1)}, u32[]{:S(2)}, u32[]{:S(2)}) collective-permute-start(f32[32,384]{1,0:T(8,128)S(1)} %shard_map.84), channel_id=1, source_target_pairs={{0,16},{8,24},{16,0},{24,8},{1,17},{9,25},{17,1},{25,9},{2,18},{10... | collective-permute-start | bytes 147464 | tf_op jit(solution)/shard_map/ppermute | solution.py:61
  92.0 6.2 %collective-permute-start.38 = (f32[32,384]{1,0:T(8,128)S(1)}, f32[32,384]{1,0:T(8,128)S(1)}, u32[]{:S(2)}, u32[]{:S(2)}) collective-permute-start(f32[32,384]{1,0:T(8,128)S(1)} %shard_map.84), channel_id=1, source_target_pairs={{0,8},{8,0},{16,24},{24,16},{1,9},{9,1},{17,25},{25,17},{2,10},{10... | collective-permute-start | bytes 147464 | tf_op jit(solution)/shard_map/ppermute | solution.py:61
  92.7 9.4 %collective-permute-start.32 = (f32[32,512]{1,0:T(8,128)S(1)}, f32[32,512]{1,0:T(8,128)S(1)}, u32[]{:S(2)}, u32[]{:S(2)}) collective-permute-start(f32[32,512]{1,0:T(8,128)S(1)} %add_add_fusion.1), channel_id=1, source_target_pairs={{0,24},{8,16},{16,8},{24,0},{1,25},{9,17},{17,9},{25,1},{2,26},{10... | collective-permute-start | bytes 196616 | tf_op jit(solution)/shard_map/ppermute | solution.py:61
  96.5 6.6 %collective-permute-start.31 = (f32[32,512]{1,0:T(8,128)S(1)}, f32[32,512]{1,0:T(8,128)S(1)}, u32[]{:S(2)}, u32[]{:S(2)}) collective-permute-start(f32[32,512]{1,0:T(8,128)S(1)} %add_add_fusion.1), channel_id=1, source_target_pairs={{0,16},{8,24},{16,0},{24,8},{1,17},{9,25},{17,1},{25,9},{2,18},{10... | collective-permute-start | bytes 196616 | tf_op jit(solution)/shard_map/ppermute | solution.py:61
  96.5 6.6 %collective-permute-start.30 = (f32[32,512]{1,0:T(8,128)S(1)}, f32[32,512]{1,0:T(8,128)S(1)}, u32[]{:S(2)}, u32[]{:S(2)}) collective-permute-start(f32[32,512]{1,0:T(8,128)S(1)} %add_add_fusion.1), channel_id=1, source_target_pairs={{0,8},{8,0},{16,24},{24,16},{1,9},{9,1},{17,25},{25,17},{2,10},{10... | collective-permute-start | bytes 196616 | tf_op jit(solution)/shard_map/ppermute | solution.py:61
  98.2 1.3 %collective-permute-start.41 = (f32[32,384]{1,0:T(8,128)S(1)}, f32[32,384]{1,0:T(8,128)S(1)}, u32[]{:S(2)}, u32[]{:S(2)}) collective-permute-start(f32[32,384]{1,0:T(8,128)S(1)} %add_add_fusion.2.own_ref), channel_id=1, source_target_pairs={{0,1},{1,0},{2,3},{3,2},{4,5},{5,4},{6,7},{7,6},{8,9},{9,8},{10,11... | collective-permute-start | bytes 147464 | tf_op jit(solution)/shard_map/ppermute | solution.py:61
  99.5 6.7 %collective-permute-start.44 = (f32[64,384]{1,0:T(8,128)S(1)}, f32[64,384]{1,0:T(8,128)S(1)}, u32[]{:S(2)}, u32[]{:S(2)}) collective-permute-start(f32[64,384]{1,0:T(8,128)S(1)} %shard_map.85.q0), channel_id=1, source_target_pairs={{0,6},{1,7},{2,4},{3,5},{4,2},{5,3},{6,0},{7,1},{8,14},{9,15},{10,... | collective-permute-start | bytes 294920 | tf_op jit(solution)/shard_map/ppermute | solution.py:61
  100.8 6.7 %collective-permute-start.43 = (f32[64,384]{1,0:T(8,128)S(1)}, f32[64,384]{1,0:T(8,128)S(1)}, u32[]{:S(2)}, u32[]{:S(2)}) collective-permute-start(f32[64,384]{1,0:T(8,128)S(1)} %shard_map.85.q0), channel_id=1, source_target_pairs={{0,4},{1,5},{2,6},{3,7},{4,0},{5,1},{6,2},{7,3},{8,12},{9,13},{10,... | collective-permute-start | bytes 294920 | tf_op jit(solution)/shard_map/ppermute | solution.py:61
  102.0 5.5 %collective-permute-start.42 = (f32[64,384]{1,0:T(8,128)S(1)}, f32[64,384]{1,0:T(8,128)S(1)}, u32[]{:S(2)}, u32[]{:S(2)}) collective-permute-start(f32[64,384]{1,0:T(8,128)S(1)} %shard_map.85.q0), channel_id=1, source_target_pairs={{0,2},{1,3},{2,0},{3,1},{4,6},{5,7},{6,4},{7,5},{8,10},{9,11},{10,... | collective-permute-start | bytes 294920 | tf_op jit(solution)/shard_map/ppermute | solution.py:61
  103.1 4.3 %collective-permute-start.33 = (f32[32,512]{1,0:T(8,128)S(1)}, f32[32,512]{1,0:T(8,128)S(1)}, u32[]{:S(2)}, u32[]{:S(2)}) collective-permute-start(f32[32,512]{1,0:T(8,128)S(1)} %add_add_fusion.mine_ref), channel_id=1, source_target_pairs={{0,1},{1,0},{2,3},{3,2},{4,5},{5,4},{6,7},{7,6},{8,9},{9,8},{10,11... | collective-permute-start | bytes 196616 | tf_op jit(solution)/shard_map/ppermute | solution.py:61
